TPU v7x, 256 devices: a whole 4x4x8 slice. The times are simulated.
256 devices in a mesh: box: 256 (over y, z, x, core).
Axes of the slice: x: 4, y: 4, z: 8, core: 2. Of those that a mesh axis runs over, the one named last changes fastest.
Arguments:
- sources: bfloat16 [128, 1048576], P(None, 'box'), may hold values from -6 to 6
- points: float32 [3, 1048576], P(None, 'box')
- near_list: int32 [2048, 12], P('box'), may hold values from 0 to 2047, as said below
- near_count: int32 [2048], P('box'), may hold values from 1 to 12
- far_list: int32 [2048, 4], P('box'), may hold values from 0 to 2047, as said below
- far_count: int32 [2048], P('box'), may hold values from 1 to 4
- leaf_basis: bfloat16 [2048, 64, 512], P('box'), may hold values from -0.25 to 0.25
- leaf_transfer: bfloat16 [256, 64, 512], P('box'), may hold values from -0.25 to 0.25
- leaf_coupling: bfloat16 [2048, 64, 256], P('box'), may hold values from -0.5 to 0.5
- branch_transfer: bfloat16 [256, 6, 64, 128], P('box'), may hold values from -1 to 1, as said below
- branch_coupling: bfloat16 [256, 7, 64, 256], P('box'), may hold values from -1 to 1, as said below
Outputs:
- field: float32 [128, 1048576], P(None, 'box')
Inputs may be any that keep to these rules, and one draw needn't show every extreme that they name: `near_list`: row b lists near_count[b] distinct leaf boxes, the first b itself, the others within 12 of b in Morton order; entries from near_count[b] on hold b and are not used. `far_list`: row b lists far_count[b] distinct leaf boxes, each 2 to 12 from b in Morton order; entries from far_count[b] on hold b and are not used. branch_transfer[d, h] is equal for all d with the same d div 2^(h+1). branch_coupling[d, h] is equal for all d with the same d div 2^h.
All inputs are finite; a program needn't handle non-finite values.
Results may differ from a plain program's by a relative error of at most 0.0031.
Values may be sent and summed in bfloat16 or wider, within the bound.
A program may use at most 64 MiB of HBM per device.

v0:
```python
import jax
import jax.numpy as jnp
from jax import lax
from jax.sharding import PartitionSpec as P

FAR_MAX = 4
REACH = 12


softening = 0.25
inverse_sphere = 0.07957747154594767
highest = lax.Precision.HIGHEST
far_offsets = (-3, -2, 2, 3)
pair_group = 4


def shifted(value, axis, steps):
    count = lax.axis_size(axis)
    first, last = (max(0, -steps), min(count, count - steps))
    return lax.ppermute(value, axis, [(source, source + steps) for source in range(first, last)])


def swapped(value, axis, apart):
    return lax.ppermute(value, axis, [(i, i ^ 1 << apart) for i in range(lax.axis_size(axis))])


def kernel_block(source_points, target_points):
    gap_x = source_points[0][:, None] - target_points[0][None, :]
    gap_y = source_points[1][:, None] - target_points[1][None, :]
    gap_z = source_points[2][:, None] - target_points[2][None, :]
    squared = gap_x * gap_x + gap_y * gap_y + gap_z * gap_z
    return (inverse_sphere / jnp.sqrt(squared + softening)).astype(jnp.bfloat16)


def move_points(payload, distance):
    return shifted(payload, "box", distance)


def move_sources(payload, distance):
    return shifted(payload, "box", distance)


def move_moments(payload, distance):
    return shifted(payload, "box", distance)


def move_branch(payload, distance):
    return shifted(payload, "box", distance)


def window(payload, mover, spread, along_axis):
    before_list = []
    for distance in range(spread, 0, -1):
        sent = payload if distance == spread else payload
        before_list.append(mover(sent, distance))
    after_list = []
    for distance in range(1, spread + 1):
        sent = payload if distance == spread else payload
        after_list.append(mover(sent, -distance))
    pieces = before_list + [payload] + after_list
    return jax.tree.map(lambda *members: jnp.concatenate(members, axis=along_axis), *pieces)


def pair_products(source_pts, target_pts, source_vals):
    kernels = jax.vmap(kernel_block, in_axes=(1, 1))(source_pts, target_pts)
    return jnp.einsum("ngp,gpq->gnq", source_vals, kernels, preferred_element_type=jnp.float32)


def on_device(
    sources,
    points,
    near_list,
    near_count,
    far_list,
    far_count,
    leaf_basis,
    leaf_transfer,
    leaf_coupling,
    branch_transfer,
    branch_coupling,
):
    leaf_count = near_count.shape[0]
    points_leaf = sources.shape[1] // leaf_count
    rhs_count = sources.shape[0]
    rank_size = leaf_basis.shape[1]
    device = lax.axis_index("box")
    devices = lax.axis_size("box")
    spread = (REACH + leaf_count - 1) // leaf_count
    first_leaf = device * leaf_count
    own_start = leaf_count + (spread - 1) * leaf_count
    window_base = first_leaf - own_start
    own_sources = sources.reshape(rhs_count, leaf_count, points_leaf)
    own_points = points.reshape(3, leaf_count, points_leaf)
    near_points = window(own_points, move_points, spread, 1)
    group_ids = jnp.arange(pair_group, dtype=jnp.int32)
    near_sources = window(own_sources, move_sources, spread, 1)
    running_ends = jnp.cumsum(near_count)
    total_pairs = running_ends[-1]

    def add_group(counter, totals):
        indices = counter * pair_group + group_ids
        in_range = indices < total_pairs
        clamped = jnp.minimum(indices, total_pairs - 1)
        targets = jnp.sum((running_ends[None, :] <= clamped[:, None]).astype(jnp.int32), axis=1)
        columns = clamped - (running_ends[targets] - near_count[targets])
        sources_at = near_list[targets, columns] - window_base
        contribs = pair_products(
            jnp.take(near_points, sources_at, axis=1),
            jnp.take(own_points, targets, axis=1),
            jnp.take(near_sources, sources_at, axis=1),
        )
        contribs = jnp.where(in_range[:, None, None], contribs, jnp.zeros((), jnp.float32))
        return totals.at[targets].add(contribs)

    rounds = (total_pairs + pair_group - 1) // pair_group
    near_sum = lax.fori_loop(
        0, rounds, add_group, jnp.zeros((leaf_count, rhs_count, points_leaf), jnp.float32)
    )
    moments = jnp.einsum(
        "krp,nkp->krn", leaf_basis, own_sources, preferred_element_type=jnp.float32
    ).astype(jnp.bfloat16)
    device_moment = jnp.dot(
        leaf_transfer[0],
        moments.reshape(leaf_count * rank_size, rhs_count),
        preferred_element_type=jnp.float32,
    )
    moment_window = window(moments, move_moments, spread, 0)
    far_columns = jnp.arange(FAR_MAX, dtype=jnp.int32)
    far_gathered = moment_window[far_list - window_base]
    far_live = far_columns[None, :] < far_count[:, None]
    far_gathered = jnp.where(far_live[:, :, None, None], far_gathered, jnp.zeros((), jnp.bfloat16))
    far_gathered = far_gathered.reshape(leaf_count, FAR_MAX * rank_size, rhs_count)
    leaf_far = jnp.einsum(
        "krq,kqn->krn", leaf_coupling, far_gathered, preferred_element_type=jnp.float32
    )
    up_levels = branch_transfer.shape[1]
    far_levels = branch_coupling.shape[1]

    def child_half(height):
        bit_value = device >> height & 1
        joined = branch_transfer[0, height].astype(jnp.float32)
        return lax.dynamic_slice_in_dim(joined, bit_value * rank_size, rank_size, 1)

    halves = [child_half(height) for height in range(up_levels)]
    levels = [device_moment]
    current = device_moment
    for height in range(up_levels):
        own_term = jnp.dot(halves[height], current, precision=highest)
        current = own_term + swapped(own_term, "box", height)
        levels.append(current)
    far_terms = []
    for height in range(far_levels):
        box_index = device >> height
        box_total = devices >> height
        received = []
        for offset in far_offsets:
            arrived = move_branch(levels[height], -offset * (1 << height))
            neighbour = box_index + offset
            usable = (neighbour >= 0) & (neighbour < box_total)
            if offset == -3:
                usable = usable & (box_index % 2 == 1)
            if offset == 3:
                usable = usable & (box_index % 2 == 0)
            received.append(jnp.where(usable, arrived, jnp.zeros((), jnp.float32)))
        coupling = branch_coupling[0, height].astype(jnp.float32)
        far_terms.append(jnp.dot(coupling, jnp.concatenate(received, axis=0), precision=highest))
    local_field = far_terms[far_levels - 1]
    for height in range(far_levels - 2, -1, -1):
        local_field = far_terms[height] + jnp.dot(halves[height].T, local_field, precision=highest)
    spread_down = jnp.dot(
        leaf_transfer[0].astype(jnp.float32).T, local_field, precision=highest
    ).reshape(leaf_count, rank_size, rhs_count)
    leaf_local = (leaf_far + spread_down).astype(jnp.bfloat16)
    far_field = jnp.einsum(
        "krn,krp->knp", leaf_local, leaf_basis, preferred_element_type=jnp.float32
    )
    combined = near_sum + far_field
    return combined.transpose(1, 0, 2).reshape(rhs_count, leaf_count * points_leaf)


def solution(mesh):
    placed = (
        P(None, "box"),
        P(None, "box"),
        P("box", None),
        P("box"),
        P("box", None),
        P("box"),
        P("box", None, None),
        P("box", None, None),
        P("box", None, None),
        P("box", None, None, None),
        P("box", None, None, None),
    )
    return jax.shard_map(
        on_device, mesh=mesh, in_specs=placed, out_specs=P(None, "box"), check_vma=False
    )
```

profile of v0, /device:TPU:86, one launch (start us, length us, event | category | flops | bytes accessed | tf_op | source)
XLA Modules:
  0.0 677.1 jit_solution(10039862904332084971)
XLA Ops:
  5.8 4.9 collective-permute-start.12
  12.7 6.0 collective-permute-start.13
  31.8 3.8 collective-permute-start.11
  36.3 4.1 collective-permute-start.4
  55.2 7.1 %collective-permute-done.7 = f32[3,8,512]{2,0,1:T(4,128)S(1)} collective-permute-done((f32[3,8,512]{2,0,1:T(4,128)S(1)}, f32[3,8,512]{2,0,1:T(4,128)S(1)}, u32[]{:S(2)}, u32[]{:S(2)}) %collective-permute-start.7) | collective-permute-done | bytes 49184 | tf_op jit(solution)/shard_map/ppermute | solution.py:20
  69.3 8.2 %collective-permute-done.20 = f32[64,128]{1,0:T(8,128)S(1)} collective-permute-done((f32[64,128]{1,0:T(8,128)S(1)}, f32[64,128]{1,0:T(8,128)S(1)}, u32[]{:S(2)}, u32[]{:S(2)}) %collective-permute-start.20) | collective-permute-done | bytes 32800 | tf_op jit(solution)/shard_map/ppermute | solution.py:20
  77.5 6.0 collective-permute-start.17
  88.1 5.1 collective-permute-done.19
  93.3 4.7 collective-permute-start.18
  100.6 20.4 %collective-permute-start.26 = (f32[64,128]{1,0:T(8,128)S(1)}, f32[64,128]{1,0:T(8,128)S(1)}, u32[]{:S(2)}, u32[]{:S(2)}) collective-permute-start(f32[64,128]{1,0:T(8,128)S(1)} %fusion.117), channel_id=1, source_target_pairs={{0,4},{1,5},{2,6},{3,7},{4,0},{5,1},{6,2},{7,3},{8,12},{9,13},{10,... | collective-permute-start | bytes 98312 | tf_op jit(solution)/shard_map/ppermute | solution.py:24
  124.3 3.7 collective-permute-start.25
  128.2 6.3 collective-permute-done.25
  134.6 5.4 collective-permute-start.22
  148.6 4.8 collective-permute-start.23
  155.0 5.7 collective-permute-start
  163.3 3.6 collective-permute-start.2
  167.0 8.0 %collective-permute-start.30 = (f32[64,128]{1,0:T(8,128)S(1)}, f32[64,128]{1,0:T(8,128)}, u32[]{:S(2)}, u32[]{:S(2)}) collective-permute-start(f32[64,128]{1,0:T(8,128)S(1)} %add.317), channel_id=1, source_target_pairs={{24,0},{25,1},{26,2},{27,3},{28,4},{29,5},{30,6},{31,7},{32,8},{33... | collective-permute-start | bytes 98312 | tf_op jit(solution)/shard_map/ppermute | solution.py:20
  175.1 8.2 %collective-permute-start.31 = (f32[64,128]{1,0:T(8,128)S(1)}, f32[64,128]{1,0:T(8,128)S(1)}, u32[]{:S(2)}, u32[]{:S(2)}) collective-permute-start(f32[64,128]{1,0:T(8,128)S(1)} %fusion.113), channel_id=1, source_target_pairs={{0,8},{1,9},{2,10},{3,11},{4,12},{5,13},{6,14},{7,15},{8,0},{9,1},... | collective-permute-start | bytes 98312 | tf_op jit(solution)/shard_map/ppermute | solution.py:24
  187.5 6.1 collective-permute-start.27
  197.4 5.9 collective-permute-start.28
  205.4 13.3 %collective-permute-start.36 = (f32[64,128]{1,0:T(8,128)S(1)}, f32[64,128]{1,0:T(8,128)S(1)}, u32[]{:S(2)}, u32[]{:S(2)}) collective-permute-start(f32[64,128]{1,0:T(8,128)S(1)} %fusion.109), channel_id=1, source_target_pairs={{0,16},{1,17},{2,18},{3,19},{4,20},{5,21},{6,22},{7,23},{8,24},{9,... | collective-permute-start | bytes 98312 | tf_op jit(solution)/shard_map/ppermute | solution.py:24
  220.6 7.5 %collective-permute-start.35 = (f32[64,128]{1,0:T(8,128)S(1)}, f32[64,128]{1,0:T(8,128)S(1)}, u32[]{:S(2)}, u32[]{:S(2)}) collective-permute-start(f32[64,128]{1,0:T(8,128)S(1)} %add.324), channel_id=1, source_target_pairs={{48,0},{49,1},{50,2},{51,3},{52,4},{53,5},{54,6},{55,7},{56,8},{57... | collective-permute-start | bytes 98312 | tf_op jit(solution)/shard_map/ppermute | solution.py:20
  231.2 7.9 %collective-permute-start.34 = (f32[64,128]{1,0:T(8,128)S(1)}, f32[64,128]{1,0:T(8,128)S(1)}, u32[]{:S(2)}, u32[]{:S(2)}) collective-permute-start(f32[64,128]{1,0:T(8,128)S(1)} %add.324), channel_id=1, source_target_pairs={{32,0},{33,1},{34,2},{35,3},{36,4},{37,5},{38,6},{39,7},{40,8},{41... | collective-permute-start | bytes 98312 | tf_op jit(solution)/shard_map/ppermute | solution.py:20
  241.4 8.5 %collective-permute-start.37 = (f32[64,128]{1,0:T(8,128)S(1)}, f32[64,128]{1,0:T(8,128)S(1)}, u32[]{:S(2)}, u32[]{:S(2)}) collective-permute-start(f32[64,128]{1,0:T(8,128)S(1)} %add.331), channel_id=1, source_target_pairs={{0,96},{1,97},{2,98},{3,99},{4,100},{5,101},{6,102},{7,103},{8,104... | collective-permute-start | bytes 98312 | tf_op jit(solution)/shard_map/ppermute | solution.py:20
  253.5 3.6 collective-permute-start.38
  257.2 10.0 %collective-permute-start.41 = (f32[64,128]{1,0:T(8,128)S(1)}, f32[64,128]{1,0:T(8,128)S(1)}, u32[]{:S(2)}, u32[]{:S(2)}) collective-permute-start(f32[64,128]{1,0:T(8,128)S(1)} %fusion.105), channel_id=1, source_target_pairs={{0,32},{1,33},{2,34},{3,35},{4,36},{5,37},{6,38},{7,39},{8,40},{9,... | collective-permute-start | bytes 98312 | tf_op jit(solution)/shard_map/ppermute | solution.py:24
  267.2 6.5 collective-permute-done.41
  277.9 14.3 %collective-permute-start.44 = (f32[64,128]{1,0:T(8,128)S(1)}, f32[64,128]{1,0:T(8,128)S(1)}, u32[]{:S(2)}, u32[]{:S(2)}) collective-permute-start(f32[64,128]{1,0:T(8,128)S(1)} %add.338), channel_id=1, source_target_pairs={{128,0},{129,1},{130,2},{131,3},{132,4},{133,5},{134,6},{135,7},{1... | collective-permute-start | bytes 98312 | tf_op jit(solution)/shard_map/ppermute | solution.py:20
  295.1 6.0 collective-permute-done.43
  326.6 8.0 %copy.28 = bf16[128,40,512]{2,0,1:T(8,128)(2,1)} copy(bf16[128,40,512]{0,2,1:T(8,128)(2,1)} %constant_dynamic-update-slice_fusion) | data formatting | bytes 10485760
  334.8 335.2 %while.13 = (s32[]{:T(128)}, f32[8,128,512]{2,1,0:T(8,128)S(1)}, s32[]{:T(128)}, s32[8]{0:T(128)S(1)}, s32[]{:T(128)}, /*index=5*/s32[]{:T(128)}, s32[8]{0:T(128...) while((s32[]{:T(128)}, f32[8,128,512]{2,1,0:T(8,128)S(1)}, ...), condition=%wide.region_4.5_spmd.clone, body=%wide.region_1.4_spmd.clone.sunk | while | flops 280770816 | bytes 6218429 | solution.py:116
  357.0 3.4 fusion.195
  371.0 3.4 fusion.195
  385.0 3.4 fusion.195
  398.9 3.4 fusion.195
  426.9 3.4 fusion.195
  440.8 3.4 fusion.195
  468.8 3.4 fusion.195
  482.7 3.4 fusion.195
  510.7 3.4 fusion.195
  524.6 3.4 fusion.195
  552.5 3.4 fusion.195
  566.5 3.4 fusion.195
  594.4 3.4 fusion.195
  608.4 3.4 fusion.195
  636.3 3.4 fusion.195
  650.3 3.4 fusion.195
  669.9 3.4 add_bitcast_fusion
  (800 shorter events, 399.9 us)
Async XLA Ops:
  3.0 21.9 %collective-permute-start.15 = (f32[64,128]{1,0:T(8,128)S(1)}, f32[64,128]{1,0:T(8,128)S(1)}, u32[]{:S(2)}, u32[]{:S(2)}) collective-permute-start(f32[64,128]{1,0:T(8,128)S(1)} %bitcast.216), channel_id=1, source_target_pairs={{3,0},{4,1},{5,2},{6,3},{7,4},{8,5},{9,6},{10,7},{11,8},{12,9},{13... | collective-permute-start | bytes 98312 | tf_op jit(solution)/shard_map/ppermute | solution.py:20
  5.8 22.1 %collective-permute-start.12 = (f32[64,128]{1,0:T(8,128)S(1)}, f32[64,128]{1,0:T(8,128)S(1)}, u32[]{:S(2)}, u32[]{:S(2)}) collective-permute-start(f32[64,128]{1,0:T(8,128)S(1)} %bitcast.217), channel_id=1, source_target_pairs={{0,3},{1,4},{2,5},{3,6},{4,7},{5,8},{6,9},{7,10},{8,11},{9,12},{10... | collective-permute-start | bytes 98312 | tf_op jit(solution)/shard_map/ppermute | solution.py:20
  10.7 21.1 %collective-permute-start.14 = (f32[64,128]{1,0:T(8,128)S(1)}, f32[64,128]{1,0:T(8,128)S(1)}, u32[]{:S(2)}, u32[]{:S(2)}) collective-permute-start(f32[64,128]{1,0:T(8,128)S(1)} %bitcast.218), channel_id=1, source_target_pairs={{2,0},{3,1},{4,2},{5,3},{6,4},{7,5},{8,6},{9,7},{10,8},{11,9},{12,... | collective-permute-start | bytes 98312 | tf_op jit(solution)/shard_map/ppermute | solution.py:20
  12.7 23.6 %collective-permute-start.13 = (f32[64,128]{1,0:T(8,128)S(1)}, f32[64,128]{1,0:T(8,128)S(1)}, u32[]{:S(2)}, u32[]{:S(2)}) collective-permute-start(f32[64,128]{1,0:T(8,128)S(1)} %bitcast.219), channel_id=1, source_target_pairs={{0,2},{1,3},{2,4},{3,5},{4,6},{5,7},{6,8},{7,9},{8,10},{9,11},{10,... | collective-permute-start | bytes 98312 | tf_op jit(solution)/shard_map/ppermute | solution.py:20
  19.5 247.6 %copy-start.11 = (bf16[1,1,64,128]{3,2,1,0:T(8,128)(2,1)}, bf16[1,1,64,128]{3,2,1,0:T(8,128)(2,1)S(1)}, u32[]{:S(2)}) copy-start(bf16[1,1,64,128]{3,2,1,0:T(8,128)(2,1)S(1)} %get-tuple-element.242) | copy-start | bytes 49156
  19.8 3.0 collective-permute-start.16
  22.8 138.6 %collective-permute-start.8 = (bf16[8,64,128]{2,1,0:T(8,128)(2,1)S(1)}, bf16[8,64,128]{2,1,0:T(8,128)(2,1)S(1)}, u32[]{:S(2)}, u32[]{:S(2)}) collective-permute-start(bf16[8,64,128]{2,1,0:T(8,128)(2,1)S(1)} %convolution_convert_fusion), channel_id=1, source_target_pairs={{0,2},{1,3},{2,4},{3,5},{4,6},{5,7},{6,8},{7,9},{8,10},{9,11},{10,... | collective-permute-start | bytes 393224 | tf_op jit(solution)/shard_map/ppermute | solution.py:20
  24.9 138.4 %collective-permute-start.9 = (bf16[8,64,128]{2,1,0:T(8,128)(2,1)S(1)}, bf16[8,64,128]{2,1,0:T(8,128)(2,1)S(1)}, u32[]{:S(2)}, u32[]{:S(2)}) collective-permute-start(bf16[8,64,128]{2,1,0:T(8,128)(2,1)S(1)} %convolution_convert_fusion), channel_id=1, source_target_pairs={{0,1},{1,2},{2,3},{3,4},{4,5},{5,6},{6,7},{7,8},{8,9},{9,10},{10,1... | collective-permute-start | bytes 393224 | tf_op jit(solution)/shard_map/ppermute | solution.py:20
  27.9 139.1 %collective-permute-start.10 = (bf16[8,64,128]{2,1,0:T(8,128)(2,1)S(1)}, bf16[8,64,128]{2,1,0:T(8,128)(2,1)S(1)}, u32[]{:S(2)}, u32[]{:S(2)}) collective-permute-start(bf16[8,64,128]{2,1,0:T(8,128)(2,1)S(1)} %convolution_convert_fusion), channel_id=1, source_target_pairs={{1,0},{2,1},{3,2},{4,3},{5,4},{6,5},{7,6},{8,7},{9,8},{10,9},{11,1... | collective-permute-start | bytes 393224 | tf_op jit(solution)/shard_map/ppermute | solution.py:20
  31.8 143.3 %collective-permute-start.11 = (bf16[8,64,128]{2,1,0:T(8,128)(2,1)S(1)}, bf16[8,64,128]{2,1,0:T(8,128)(2,1)S(1)}, u32[]{:S(2)}, u32[]{:S(2)}) collective-permute-start(bf16[8,64,128]{2,1,0:T(8,128)(2,1)S(1)} %convolution_convert_fusion), channel_id=1, source_target_pairs={{2,0},{3,1},{4,2},{5,3},{6,4},{7,5},{8,6},{9,7},{10,8},{11,9},{12,... | collective-permute-start | bytes 393224 | tf_op jit(solution)/shard_map/ppermute | solution.py:20
  36.3 6.1 collective-permute-start.4
  42.4 5.6 collective-permute-start.5
  48.0 4.7 collective-permute-start.6
  51.2 261.3 %copy-start.4 = (bf16[1,64,512]{2,1,0:T(8,128)(2,1)S(1)}, bf16[1,64,512]{2,1,0:T(8,128)(2,1)}, u32[]{:S(2)}) copy-start(bf16[1,64,512]{2,1,0:T(8,128)(2,1)} %param.20) | copy-start | bytes 196612
  52.7 9.6 %collective-permute-start.7 = (f32[3,8,512]{2,0,1:T(4,128)S(1)}, f32[3,8,512]{2,0,1:T(4,128)S(1)}, u32[]{:S(2)}, u32[]{:S(2)}) collective-permute-start(f32[3,8,512]{2,0,1:T(4,128)S(1)} %bitcast.210), channel_id=1, source_target_pairs={{2,0},{3,1},{4,2},{5,3},{6,4},{7,5},{8,6},{9,7},{10,8},{11,9},{12,... | collective-permute-start | bytes 147464 | tf_op jit(solution)/shard_map/ppermute | solution.py:20
  62.3 3.9 collective-permute-start.21
  66.3 11.2 %collective-permute-start.20 = (f32[64,128]{1,0:T(8,128)S(1)}, f32[64,128]{1,0:T(8,128)S(1)}, u32[]{:S(2)}, u32[]{:S(2)}) collective-permute-start(f32[64,128]{1,0:T(8,128)S(1)} %add.303), channel_id=1, source_target_pairs={{6,0},{7,1},{8,2},{9,3},{10,4},{11,5},{12,6},{13,7},{14,8},{15,9},... | collective-permute-start | bytes 98312 | tf_op jit(solution)/shard_map/ppermute | solution.py:20
  77.5 7.6 %collective-permute-start.17 = (f32[64,128]{1,0:T(8,128)S(1)}, f32[64,128]{1,0:T(8,128)S(1)}, u32[]{:S(2)}, u32[]{:S(2)}) collective-permute-start(f32[64,128]{1,0:T(8,128)S(1)} %add.303), channel_id=1, source_target_pairs={{0,6},{1,7},{2,8},{3,9},{4,10},{5,11},{6,12},{7,13},{8,14},{9,15},... | collective-permute-start | bytes 98312 | tf_op jit(solution)/shard_map/ppermute | solution.py:20
  85.1 8.2 %collective-permute-start.19 = (f32[64,128]{1,0:T(8,128)S(1)}, f32[64,128]{1,0:T(8,128)S(1)}, u32[]{:S(2)}, u32[]{:S(2)}) collective-permute-start(f32[64,128]{1,0:T(8,128)S(1)} %add.303), channel_id=1, source_target_pairs={{4,0},{5,1},{6,2},{7,3},{8,4},{9,5},{10,6},{11,7},{12,8},{13,9},{1... | collective-permute-start | bytes 98312 | tf_op jit(solution)/shard_map/ppermute | solution.py:20
  93.3 7.3 %collective-permute-start.18 = (f32[64,128]{1,0:T(8,128)S(1)}, f32[64,128]{1,0:T(8,128)S(1)}, u32[]{:S(2)}, u32[]{:S(2)}) collective-permute-start(f32[64,128]{1,0:T(8,128)S(1)} %add.303), channel_id=1, source_target_pairs={{0,4},{1,5},{2,6},{3,7},{4,8},{5,9},{6,10},{7,11},{8,12},{9,13},{1... | collective-permute-start | bytes 98312 | tf_op jit(solution)/shard_map/ppermute | solution.py:20
  100.6 23.7 %collective-permute-start.26 = (f32[64,128]{1,0:T(8,128)S(1)}, f32[64,128]{1,0:T(8,128)S(1)}, u32[]{:S(2)}, u32[]{:S(2)}) collective-permute-start(f32[64,128]{1,0:T(8,128)S(1)} %fusion.117), channel_id=1, source_target_pairs={{0,4},{1,5},{2,6},{3,7},{4,0},{5,1},{6,2},{7,3},{8,12},{9,13},{10,... | collective-permute-start | bytes 98312 | tf_op jit(solution)/shard_map/ppermute | solution.py:24
  124.3 10.3 %collective-permute-start.25 = (f32[64,128]{1,0:T(8,128)S(1)}, f32[64,128]{1,0:T(8,128)S(1)}, u32[]{:S(2)}, u32[]{:S(2)}) collective-permute-start(f32[64,128]{1,0:T(8,128)S(1)} %add.310), channel_id=1, source_target_pairs={{12,0},{13,1},{14,2},{15,3},{16,4},{17,5},{18,6},{19,7},{20,8},{21... | collective-permute-start | bytes 98312 | tf_op jit(solution)/shard_map/ppermute | solution.py:20
  134.6 8.2 %collective-permute-start.22 = (f32[64,128]{1,0:T(8,128)S(1)}, f32[64,128]{1,0:T(8,128)S(1)}, u32[]{:S(2)}, u32[]{:S(2)}) collective-permute-start(f32[64,128]{1,0:T(8,128)S(1)} %add.310), channel_id=1, source_target_pairs={{0,12},{1,13},{2,14},{3,15},{4,16},{5,17},{6,18},{7,19},{8,20},{9,... | collective-permute-start | bytes 98312 | tf_op jit(solution)/shard_map/ppermute | solution.py:20
  142.8 5.8 collective-permute-start.24
  148.6 6.4 collective-permute-start.23
  155.0 162.5 %collective-permute-start = (bf16[128,8,512]{0,2,1:T(8,128)(2,1)S(1)}, bf16[128,8,512]{0,2,1:T(8,128)(2,1)}, u32[]{:S(2)}, u32[]{:S(2)}) collective-permute-start(bf16[128,8,512]{0,2,1:T(8,128)(2,1)S(1)} %bitcast.197), channel_id=1, source_target_pairs={{0,2},{1,3},{2,4},{3,5},{4,6},{5,7},{6,8},{7,9},{8,10},{9,11},{10,... | collective-permute-start | bytes 3145736 | tf_op jit(solution)/shard_map/ppermute | solution.py:20
  161.4 158.4 %collective-permute-start.1 = (bf16[128,8,512]{0,2,1:T(8,128)(2,1)S(1)}, bf16[128,8,512]{0,2,1:T(8,128)(2,1)}, u32[]{:S(2)}, u32[]{:S(2)}) collective-permute-start(bf16[128,8,512]{0,2,1:T(8,128)(2,1)S(1)} %bitcast.198), channel_id=1, source_target_pairs={{0,1},{1,2},{2,3},{3,4},{4,5},{5,6},{6,7},{7,8},{8,9},{9,10},{10,1... | collective-permute-start | bytes 3145736 | tf_op jit(solution)/shard_map/ppermute | solution.py:20
  163.3 159.9 %collective-permute-start.2 = (bf16[128,8,512]{0,2,1:T(8,128)(2,1)S(1)}, bf16[128,8,512]{0,2,1:T(8,128)(2,1)}, u32[]{:S(2)}, u32[]{:S(2)}) collective-permute-start(bf16[128,8,512]{0,2,1:T(8,128)(2,1)S(1)} %bitcast.199), channel_id=1, source_target_pairs={{1,0},{2,1},{3,2},{4,3},{5,4},{6,5},{7,6},{8,7},{9,8},{10,9},{11,1... | collective-permute-start | bytes 3145736 | tf_op jit(solution)/shard_map/ppermute | solution.py:20
  167.0 27.6 %collective-permute-start.30 = (f32[64,128]{1,0:T(8,128)S(1)}, f32[64,128]{1,0:T(8,128)}, u32[]{:S(2)}, u32[]{:S(2)}) collective-permute-start(f32[64,128]{1,0:T(8,128)S(1)} %add.317), channel_id=1, source_target_pairs={{24,0},{25,1},{26,2},{27,3},{28,4},{29,5},{30,6},{31,7},{32,8},{33... | collective-permute-start | bytes 98312 | tf_op jit(solution)/shard_map/ppermute | solution.py:20
  175.1 11.8 %collective-permute-start.31 = (f32[64,128]{1,0:T(8,128)S(1)}, f32[64,128]{1,0:T(8,128)S(1)}, u32[]{:S(2)}, u32[]{:S(2)}) collective-permute-start(f32[64,128]{1,0:T(8,128)S(1)} %fusion.113), channel_id=1, source_target_pairs={{0,8},{1,9},{2,10},{3,11},{4,12},{5,13},{6,14},{7,15},{8,0},{9,1},... | collective-permute-start | bytes 98312 | tf_op jit(solution)/shard_map/ppermute | solution.py:24
  187.5 9.9 %collective-permute-start.27 = (f32[64,128]{1,0:T(8,128)S(1)}, f32[64,128]{1,0:T(8,128)S(1)}, u32[]{:S(2)}, u32[]{:S(2)}) collective-permute-start(f32[64,128]{1,0:T(8,128)S(1)} %add.317), channel_id=1, source_target_pairs={{0,24},{1,25},{2,26},{3,27},{4,28},{5,29},{6,30},{7,31},{8,32},{9,... | collective-permute-start | bytes 98312 | tf_op jit(solution)/shard_map/ppermute | solution.py:20
  194.6 8.8 %collective-permute-start.29 = (f32[64,128]{1,0:T(8,128)S(1)}, f32[64,128]{1,0:T(8,128)S(1)}, u32[]{:S(2)}, u32[]{:S(2)}) collective-permute-start(f32[64,128]{1,0:T(8,128)S(1)} %add.317), channel_id=1, source_target_pairs={{16,0},{17,1},{18,2},{19,3},{20,4},{21,5},{22,6},{23,7},{24,8},{25... | collective-permute-start | bytes 98312 | tf_op jit(solution)/shard_map/ppermute | solution.py:20
  197.4 7.9 %collective-permute-start.28 = (f32[64,128]{1,0:T(8,128)S(1)}, f32[64,128]{1,0:T(8,128)S(1)}, u32[]{:S(2)}, u32[]{:S(2)}) collective-permute-start(f32[64,128]{1,0:T(8,128)S(1)} %add.317), channel_id=1, source_target_pairs={{0,16},{1,17},{2,18},{3,19},{4,20},{5,21},{6,22},{7,23},{8,24},{9,... | collective-permute-start | bytes 98312 | tf_op jit(solution)/shard_map/ppermute | solution.py:20
  203.4 25.0 %collective-permute-start.32 = (f32[64,128]{1,0:T(8,128)S(1)}, f32[64,128]{1,0:T(8,128)S(1)}, u32[]{:S(2)}, u32[]{:S(2)}) collective-permute-start(f32[64,128]{1,0:T(8,128)S(1)} %add.324), channel_id=1, source_target_pairs={{0,48},{1,49},{2,50},{3,51},{4,52},{5,53},{6,54},{7,55},{8,56},{9,... | collective-permute-start | bytes 98312 | tf_op jit(solution)/shard_map/ppermute | solution.py:20
  205.4 15.3 %collective-permute-start.36 = (f32[64,128]{1,0:T(8,128)S(1)}, f32[64,128]{1,0:T(8,128)S(1)}, u32[]{:S(2)}, u32[]{:S(2)}) collective-permute-start(f32[64,128]{1,0:T(8,128)S(1)} %fusion.109), channel_id=1, source_target_pairs={{0,16},{1,17},{2,18},{3,19},{4,20},{5,21},{6,22},{7,23},{8,24},{9,... | collective-permute-start | bytes 98312 | tf_op jit(solution)/shard_map/ppermute | solution.py:24
  220.6 10.6 %collective-permute-start.35 = (f32[64,128]{1,0:T(8,128)S(1)}, f32[64,128]{1,0:T(8,128)S(1)}, u32[]{:S(2)}, u32[]{:S(2)}) collective-permute-start(f32[64,128]{1,0:T(8,128)S(1)} %add.324), channel_id=1, source_target_pairs={{48,0},{49,1},{50,2},{51,3},{52,4},{53,5},{54,6},{55,7},{56,8},{57... | collective-permute-start | bytes 98312 | tf_op jit(solution)/shard_map/ppermute | solution.py:20
  228.4 10.9 %collective-permute-start.33 = (f32[64,128]{1,0:T(8,128)S(1)}, f32[64,128]{1,0:T(8,128)S(1)}, u32[]{:S(2)}, u32[]{:S(2)}) collective-permute-start(f32[64,128]{1,0:T(8,128)S(1)} %add.324), channel_id=1, source_target_pairs={{0,32},{1,33},{2,34},{3,35},{4,36},{5,37},{6,38},{7,39},{8,40},{9,... | collective-permute-start | bytes 98312 | tf_op jit(solution)/shard_map/ppermute | solution.py:20
  231.2 10.3 %collective-permute-start.34 = (f32[64,128]{1,0:T(8,128)S(1)}, f32[64,128]{1,0:T(8,128)S(1)}, u32[]{:S(2)}, u32[]{:S(2)}) collective-permute-start(f32[64,128]{1,0:T(8,128)S(1)} %add.324), channel_id=1, source_target_pairs={{32,0},{33,1},{34,2},{35,3},{36,4},{37,5},{38,6},{39,7},{40,8},{41... | collective-permute-start | bytes 98312 | tf_op jit(solution)/shard_map/ppermute | solution.py:20
  239.3 10.7 %collective-permute-start.40 = (f32[64,128]{1,0:T(8,128)S(1)}, f32[64,128]{1,0:T(8,128)S(1)}, u32[]{:S(2)}, u32[]{:S(2)}) collective-permute-start(f32[64,128]{1,0:T(8,128)S(1)} %add.331), channel_id=1, source_target_pairs={{96,0},{97,1},{98,2},{99,3},{100,4},{101,5},{102,6},{103,7},{104,8... | collective-permute-start | bytes 98312 | tf_op jit(solution)/shard_map/ppermute | solution.py:20
  241.4 12.1 %collective-permute-start.37 = (f32[64,128]{1,0:T(8,128)S(1)}, f32[64,128]{1,0:T(8,128)S(1)}, u32[]{:S(2)}, u32[]{:S(2)}) collective-permute-start(f32[64,128]{1,0:T(8,128)S(1)} %add.331), channel_id=1, source_target_pairs={{0,96},{1,97},{2,98},{3,99},{4,100},{5,101},{6,102},{7,103},{8,104... | collective-permute-start | bytes 98312 | tf_op jit(solution)/shard_map/ppermute | solution.py:20
  250.0 7.2 %collective-permute-start.39 = (f32[64,128]{1,0:T(8,128)S(1)}, f32[64,128]{1,0:T(8,128)S(1)}, u32[]{:S(2)}, u32[]{:S(2)}) collective-permute-start(f32[64,128]{1,0:T(8,128)S(1)} %add.331), channel_id=1, source_target_pairs={{64,0},{65,1},{66,2},{67,3},{68,4},{69,5},{70,6},{71,7},{72,8},{73... | collective-permute-start | bytes 98312 | tf_op jit(solution)/shard_map/ppermute | solution.py:20
  253.5 22.9 %collective-permute-start.38 = (f32[64,128]{1,0:T(8,128)S(1)}, f32[64,128]{1,0:T(8,128)S(1)}, u32[]{:S(2)}, u32[]{:S(2)}) collective-permute-start(f32[64,128]{1,0:T(8,128)S(1)} %add.331), channel_id=1, source_target_pairs={{0,64},{1,65},{2,66},{3,67},{4,68},{5,69},{6,70},{7,71},{8,72},{9,... | collective-permute-start | bytes 98312 | tf_op jit(solution)/shard_map/ppermute | solution.py:20
  257.2 16.5 %collective-permute-start.41 = (f32[64,128]{1,0:T(8,128)S(1)}, f32[64,128]{1,0:T(8,128)S(1)}, u32[]{:S(2)}, u32[]{:S(2)}) collective-permute-start(f32[64,128]{1,0:T(8,128)S(1)} %fusion.105), channel_id=1, source_target_pairs={{0,32},{1,33},{2,34},{3,35},{4,36},{5,37},{6,38},{7,39},{8,40},{9,... | collective-permute-start | bytes 98312 | tf_op jit(solution)/shard_map/ppermute | solution.py:24
  273.7 51.8 %collective-permute-start.3 = (bf16[128,8,512]{0,2,1:T(8,128)(2,1)S(1)}, bf16[128,8,512]{0,2,1:T(8,128)(2,1)S(1)}, u32[]{:S(2)}, u32[]{:S(2)}) collective-permute-start(bf16[128,8,512]{0,2,1:T(8,128)(2,1)S(1)} %bitcast.200), channel_id=1, source_target_pairs={{2,0},{3,1},{4,2},{5,3},{6,4},{7,5},{8,6},{9,7},{10,8},{11,9},{12,... | collective-permute-start | bytes 3145736 | tf_op jit(solution)/shard_map/ppermute | solution.py:20
  276.5 0.7 collective-permute-start.42
  277.2 0.7 collective-permute-start.45
  277.9 15.9 %collective-permute-start.44 = (f32[64,128]{1,0:T(8,128)S(1)}, f32[64,128]{1,0:T(8,128)S(1)}, u32[]{:S(2)}, u32[]{:S(2)}) collective-permute-start(f32[64,128]{1,0:T(8,128)S(1)} %add.338), channel_id=1, source_target_pairs={{128,0},{129,1},{130,2},{131,3},{132,4},{133,5},{134,6},{135,7},{1... | collective-permute-start | bytes 98312 | tf_op jit(solution)/shard_map/ppermute | solution.py:20
  293.7 7.3 %collective-permute-start.43 = (f32[64,128]{1,0:T(8,128)S(1)}, f32[64,128]{1,0:T(8,128)S(1)}, u32[]{:S(2)}, u32[]{:S(2)}) collective-permute-start(f32[64,128]{1,0:T(8,128)S(1)} %add.338), channel_id=1, source_target_pairs={{0,128},{1,129},{2,130},{3,131},{4,132},{5,133},{6,134},{7,135},{8... | collective-permute-start | bytes 98312 | tf_op jit(solution)/shard_map/ppermute | solution.py:20
  (18 other events, 1770.0 us)
where the time goes:
time: 688 us; the launch traced here: 677 us
  starting transfers between devices  211 us (31%)
  local copies, waits for them, and re-layouts  202 us (29%)
  matrix products  99 us (14%)
  other arithmetic  92 us (13%)
  waiting for transfers between devices  67.3 us (10%)
    ppermute x40, starting transfers between devices, shifted(): lax.ppermute(value, axis, [(source, source + steps) for source in range(f...  159 us
    dot_general x24, matrix products, pair_products(): jnp.einsum('ngp,gpq->gnq', source_vals, kernels, preferred_element_type=j...  81.3 us
    gather x24, local copies, waits for them, and re-layouts, add_group(): jnp.take(near_sources, sources_at, axis=1)  73.6 us
    scatter-add x24, other arithmetic, add_group(): return totals.at[targets].add(contribs)  54.5 us
    ppermute x6, starting transfers between devices, swapped(): lax.ppermute(value, axis, [(i, i ^ 1 << apart) for i in range(lax.axis_si...  52 us
    ppermute x40, waiting for transfers between devices, shifted(): lax.ppermute(value, axis, [(source, source + steps) for source in range(f...  50.4 us
    gather x24, local copies, waits for them, and re-layouts, add_group(): jnp.take(near_points, sources_at, axis=1)  37.2 us
    gather x48, local copies, waits for them, and re-layouts, add_group(): columns = clamped - (running_ends[targets] - near_count[targets])  30.7 us
  transfers between devices with their start and end apart: 46, of which 23 were waited for; matrix products, arithmetic and copies ran while one was open for 6% of the time, Pallas kernels for 0%

commit v1 on v0

v1 whole, which is shorter than its diff:
```python
import functools

import jax
import jax.numpy as jnp
from jax import lax
from jax.experimental import pallas as pl
from jax.experimental.pallas import tpu as pltpu
from jax.sharding import PartitionSpec as P

F32 = jnp.float32
BF16 = jnp.bfloat16
SOFT = 0.25
INV = 0.07957747154594767
SCALE = 1.0 / INV
EXTENT = 1024.0 * SCALE * SCALE
FAR_SCALE = 1e-27
LEAF = 8
PTS = 512
RANK = 64
RHS = 128
NEAR = 12
FAR = 4
REACH = 12
SLOTS = LEAF + 2 * REACH
OWN = REACH
UP = 6
LEVELS = 7
FEAT = 32
GROUP = 6
MESH = pl.DeviceIdType.MESH

WINDOW = (
    (1, 6, 2, 0),
    (-1, 0, 2, 0),
    (1, 4, 2, 1),
    (-1, 2, 2, 1),
    (2, 4, 4, 2),
    (-2, 0, 4, 2),
    (1, 0, 4, 2),
    (-1, 4, 4, 2),
)
EDGES = ((1, 0, 8), (-1, 0, 8), (2, 4, 4), (-2, 0, 4))
N_WIN, N_EDGE = len(WINDOW), len(EDGES)
I_PTS = 0
I_MOM = I_PTS + N_EDGE
I_WIN = I_MOM + N_EDGE
I_SWAP = I_WIN + N_WIN
I_FAR = I_SWAP + UP
N_MSG = I_FAR + 3 * LEVELS

UP_AT = (0, 1, 3, 5, 7, 10)
FAR_AT = (11, 11, 12, 12, 13, 14)


def split3(x):
    a = x.astype(BF16)
    r = x - a.astype(F32)
    b = r.astype(BF16)
    return a, b, (r - b.astype(F32)).astype(BF16)


def rows(parts):
    return jnp.concatenate(parts, axis=0)


def source_features(x):
    n = jnp.sum(x * x, axis=0, keepdims=True)
    a, b, c = split3(x)
    n0, n1, n2 = split3(n + SOFT * SCALE * SCALE)
    ones = jnp.ones((3, PTS), BF16)
    return rows([a, b, a, b, c, a, n0, n1, n2, ones, jnp.zeros((FEAT - 24, PTS), BF16)]), n


def target_features(x):
    n = jnp.sum(x * x, axis=0, keepdims=True)
    a, b, c = split3(-2.0 * x)
    n0, n1, n2 = split3(n)
    ones = jnp.ones((3, PTS), BF16)
    return rows([a, a, b, b, a, c, ones, n0, n1, n2, jnp.zeros((FEAT - 24, PTS), BF16)])


def exact_dot(left, right, contract=1):
    high = right.astype(BF16)
    low = (right - high.astype(F32)).astype(BF16)
    both = lax.dot_general(
        left,
        jnp.concatenate([high, low], axis=1),
        (((contract,), (0,)), ((), ())),
        preferred_element_type=F32,
    )
    return both[:, :RHS] + both[:, RHS:]


def tree_kernel(
    devices,
    near_list,
    near_count,
    far_list,
    far_count,
    sources,
    points,
    basis_in,
    leaf_transfer_in,
    coupling_in,
    branch_transfer_in,
    branch_coupling_in,
    field,
    leaf_local_out,
    norms_out,
    charges_out,
    points_out,
    charges,
    pts,
    moments,
    feats,
    kernels,
    basis,
    transfer,
    coupling,
    branch_t,
    branch_c,
    level,
    term,
    swapped,
    arrived,
    far,
    spread,
    norms,
    leaf_local,
    out_buf,
    load_sem,
    store_sem,
    send_sem,
    recv_sem,
):
    me = lax.axis_index("box")

    def other(distance):
        return lax.rem(me + distance + devices, devices)

    def third(height):
        odd = lax.rem(lax.div(me, 1 << height), 2)
        return other((3 - 6 * odd) * (1 << height))

    def remote(index, src, dst, device):
        return pltpu.make_async_remote_copy(
            src_ref=src,
            dst_ref=dst,
            send_sem=send_sem.at[index],
            recv_sem=recv_sem.at[index],
            device_id=(device,),
            device_id_type=MESH,
        )

    barrier = pltpu.get_barrier_semaphore()
    partners = [other(s * (1 << k)) for k in range(LEVELS) for s in (1, -1)]
    partners += [other(devices // 2)] + [third(h) for h in range(LEVELS)]
    for partner in partners:
        pl.semaphore_signal(barrier, inc=1, device_id=(partner,), device_id_type=MESH)

    loads = []

    def load(src, dst):
        copy = pltpu.make_async_copy(src, dst, load_sem.at[len(loads)])
        copy.start()
        loads.append(copy)
        return copy

    load_points = [load(points.at[:, pl.ds(i * PTS, PTS)], pts.at[OWN + i]) for i in range(LEAF)]
    load_charges = [
        load(sources.at[:, pl.ds(i * PTS, PTS)], charges.at[OWN + i]) for i in range(LEAF)
    ]
    load_basis = load(basis_in, basis)
    load_transfer = load(leaf_transfer_in.at[0], transfer)
    load_branch_t = load(branch_transfer_in.at[0], branch_t)
    load_branch_c = load(branch_coupling_in.at[0], branch_c)
    load_coupling = load(coupling_in, coupling)

    def edge(base, buf, which):
        distance, first, count = EDGES[which]
        return remote(
            base + which,
            buf.at[pl.ds(OWN + first, count)],
            buf.at[pl.ds(OWN + first - LEAF * distance, count)],
            other(distance),
        )

    def window(which):
        distance, first, count, _ = WINDOW[which]
        return remote(
            I_WIN + which,
            charges.at[pl.ds(OWN + first, count)],
            charges.at[pl.ds(OWN + first - LEAF * distance, count)],
            other(distance),
        )

    def window_stage(stage):
        for which in range(N_WIN):
            if WINDOW[which][3] == stage:
                window(which).start()

    def swap(height):
        bit = lax.rem(lax.div(me, 1 << height), 2)
        return remote(
            I_SWAP + height,
            term.at[height],
            swapped.at[height],
            me + (1 - 2 * bit) * (1 << height),
        )

    def far_copies(height):
        step = 1 << height
        copies = []
        for slot, device in ((0, other(2 * step)), (1, other(-2 * step)), (2, third(height))):
            if height == LEVELS - 1 and slot == 1:
                continue
            copies.append(
                remote(I_FAR + 3 * height + slot, level.at[height], arrived.at[height, slot], device)
            )
        return copies

    def half(height):
        bit = lax.rem(lax.div(me, 1 << height), 2)
        joined = branch_t[height].astype(F32)
        return jnp.where(bit == 1, joined[:, RANK:], joined[:, :RANK]).astype(BF16)

    for copy in load_points:
        copy.wait()
    pl.semaphore_wait(barrier, len(partners))
    for which in range(N_EDGE):
        edge(I_PTS, pts, which).start()
    for copy in load_charges:
        copy.wait()
    window_stage(0)

    load_basis.wait()
    load_transfer.wait()
    for i in range(LEAF):
        moments[OWN + i] = lax.dot_general(
            basis[i], charges[OWN + i], (((1,), (1,)), ((), ())), preferred_element_type=F32
        ).astype(BF16)
    level[0] = jnp.dot(
        transfer[...],
        moments[pl.ds(OWN, LEAF)].reshape(LEAF * RANK, RHS),
        preferred_element_type=F32,
    )
    load_branch_t.wait()
    term[0] = exact_dot(half(0), level[0])
    swap(0).start()
    for which in range(N_EDGE):
        edge(I_MOM, moments, which).start()
    for copy in far_copies(0):
        copy.start()

    def prepare(slot):
        x = pts[slot]
        centred = (x - x[:, 0:1]) * SCALE
        packed, own_norm = source_features(centred)
        feats[slot] = packed.astype(F32).T.astype(BF16)
        apart = (x - pts[OWN][:, 0:1]) * SCALE
        apart_norm = jnp.sum(apart * apart, axis=0, keepdims=True) * FAR_SCALE
        norms[pl.ds(slot, 1)] = jnp.maximum(own_norm, apart_norm)

    def prepare_pair(i, carry):
        prepare(2 * i)
        prepare(2 * i + 1)
        return carry

    lax.fori_loop(OWN // 2, (OWN + LEAF) // 2, prepare_pair, 0)
    for which in range(N_EDGE):
        edge(I_PTS, pts, which).wait_recv()
    lax.fori_loop(0, OWN // 2, prepare_pair, 0)
    lax.fori_loop((OWN + LEAF) // 2, SLOTS // 2, prepare_pair, 0)

    def slot_of(entry):
        return jnp.clip(entry - me * LEAF + OWN, 0, SLOTS - 1)

    def build(leaf, column):
        slot = slot_of(near_list[leaf, column])
        target = (pts[OWN + leaf] - pts[slot][:, 0:1]) * SCALE
        squared = jnp.dot(feats[slot], target_features(target), preferred_element_type=F32)
        kernels[leaf * NEAR + column] = lax.rsqrt(
            jnp.maximum(squared, SOFT * SCALE * SCALE)
        ).astype(BF16)

    def up_step(height):
        swap(height).wait_recv()
        level[height + 1] = term[height] + swapped[height]
        if height + 1 < UP:
            term[height + 1] = exact_dot(half(height + 1), level[height + 1])
            swap(height + 1).start()
        for copy in far_copies(height + 1):
            copy.start()
        if height < 2:
            window_stage(height + 1)

    def far_step(height):
        for copy in far_copies(height):
            copy.wait_recv()
        index = lax.div(me, 1 << height)
        total = devices >> height
        odd = lax.rem(index, 2)

        def kept(slot, usable):
            return jnp.where(usable, arrived[height, slot], 0.0)

        last = 0 if height == LEVELS - 1 else 1
        stack = rows(
            [
                kept(2, (odd == 1) & (index >= 3)),
                kept(0, index >= 2),
                kept(last, index + 2 < total),
                kept(2, (odd == 0) & (index + 3 < total)),
            ]
        )
        far[height] = exact_dot(branch_c[height], stack)

    def near_group(group, carry):
        leaf = lax.div(group, NEAR // GROUP)
        first = lax.rem(group, NEAR // GROUP) * GROUP
        for u in range(GROUP):
            build(leaf, first + u)
        for height, at in enumerate(UP_AT):

            @pl.when(group == at)
            def _():
                up_step(height)

        for height, at in enumerate(FAR_AT):

            @pl.when(group == at)
            def _():
                if height == 0:
                    load_branch_c.wait()
                far_step(height)

        return carry

    lax.fori_loop(0, LEAF * NEAR // GROUP, near_group, 0)

    far_step(LEVELS - 1)
    local = far[LEVELS - 1]
    for height in range(UP - 1, -1, -1):
        local = far[height] + exact_dot(half(height), local, 0)
    spread[...] = exact_dot(transfer[...], local, 0).reshape(LEAF, RANK, RHS)
    load_coupling.wait()
    for which in range(N_EDGE):
        edge(I_MOM, moments, which).wait_recv()
    for which in range(N_WIN):
        window(which).wait_recv()
    keep = [
        pltpu.make_async_copy(charges, charges_out, store_sem.at[2]),
        pltpu.make_async_copy(pts, points_out, store_sem.at[3]),
        pltpu.make_async_copy(norms, norms_out, store_sem.at[4]),
    ]
    for copy in keep:
        copy.start()

    def out_copy(leaf, buf):
        return pltpu.make_async_copy(
            out_buf.at[buf], field.at[:, pl.ds(pl.multiple_of(leaf * PTS, PTS), PTS)], store_sem.at[buf]
        )

    def finish(leaf, buf):
        blocks = []
        for j in range(FAR):
            block = moments[slot_of(far_list[leaf, j])]
            blocks.append(jnp.where(j < far_count[leaf], block.astype(F32), 0.0).astype(BF16))
        here = jnp.dot(coupling[leaf], rows(blocks), preferred_element_type=F32) + spread[leaf]
        here = here.astype(BF16)
        leaf_local[leaf] = here
        total = lax.dot_general(
            here, basis[leaf], (((0,), (0,)), ((), ())), preferred_element_type=F32
        )
        for j in range(NEAR):
            block = charges[slot_of(near_list[leaf, j])]
            block = jnp.where(j < near_count[leaf], block, jnp.zeros_like(block))
            total += jnp.dot(block, kernels[leaf * NEAR + j], preferred_element_type=F32)
        out_buf[buf] = total
        out_copy(leaf, buf).start()

    def finish_pair(i, carry):
        for buf in range(2):

            @pl.when(i > 0)
            def _():
                out_copy(2 * i - 2 + buf, buf).wait()

            finish(2 * i + buf, buf)
        return carry

    lax.fori_loop(0, LEAF // 2, finish_pair, 0)
    out_copy(LEAF - 2, 0).wait()
    out_copy(LEAF - 1, 1).wait()
    keep.append(pltpu.make_async_copy(leaf_local, leaf_local_out, store_sem.at[5]))
    keep[-1].start()
    for copy in keep:
        copy.wait()
    for which in range(N_EDGE):
        edge(I_PTS, pts, which).wait_send()
        edge(I_MOM, moments, which).wait_send()
    for which in range(N_WIN):
        window(which).wait_send()
    for height in range(UP):
        swap(height).wait_send()
    for height in range(LEVELS):
        for copy in far_copies(height):
            copy.wait_send()


N_LOAD = 2 * LEAF + 5


def tree(devices, *operands):
    any_spec = pl.BlockSpec(memory_space=pl.ANY)
    smem_spec = pl.BlockSpec(memory_space=pltpu.SMEM)
    return pl.pallas_call(
        functools.partial(tree_kernel, devices),
        out_shape=(
            jax.ShapeDtypeStruct((RHS, LEAF * PTS), F32),
            jax.ShapeDtypeStruct((LEAF, RANK, RHS), BF16),
            jax.ShapeDtypeStruct((SLOTS, PTS), F32),
            jax.ShapeDtypeStruct((SLOTS, RHS, PTS), BF16),
            jax.ShapeDtypeStruct((SLOTS, 3, PTS), F32),
        ),
        in_specs=[smem_spec] * 4 + [any_spec] * 7,
        out_specs=(any_spec,) * 5,
        scratch_shapes=[
            pltpu.VMEM((SLOTS, RHS, PTS), BF16),
            pltpu.VMEM((SLOTS, 3, PTS), F32),
            pltpu.VMEM((SLOTS, RANK, RHS), BF16),
            pltpu.VMEM((SLOTS, PTS, FEAT), BF16),
            pltpu.VMEM((LEAF * NEAR, PTS, PTS), BF16),
            pltpu.VMEM((LEAF, RANK, PTS), BF16),
            pltpu.VMEM((RANK, LEAF * RANK), BF16),
            pltpu.VMEM((LEAF, RANK, FAR * RANK), BF16),
            pltpu.VMEM((UP, RANK, 2 * RANK), BF16),
            pltpu.VMEM((LEVELS, RANK, 4 * RANK), BF16),
            pltpu.VMEM((LEVELS, RANK, RHS), F32),
            pltpu.VMEM((UP, RANK, RHS), F32),
            pltpu.VMEM((UP, RANK, RHS), F32),
            pltpu.VMEM((LEVELS, 3, RANK, RHS), F32),
            pltpu.VMEM((LEVELS, RANK, RHS), F32),
            pltpu.VMEM((LEAF, RANK, RHS), F32),
            pltpu.VMEM((SLOTS, PTS), F32),
            pltpu.VMEM((LEAF, RANK, RHS), BF16),
            pltpu.VMEM((2, RHS, PTS), F32),
            pltpu.SemaphoreType.DMA((N_LOAD,)),
            pltpu.SemaphoreType.DMA((6,)),
            pltpu.SemaphoreType.DMA((N_MSG,)),
            pltpu.SemaphoreType.DMA((N_MSG,)),
        ],
        compiler_params=pltpu.CompilerParams(
            collective_id=0, has_side_effects=True, vmem_limit_bytes=66_000_000
        ),
        name="tree",
    )(*operands)


def result_kernel(
    near_list, near_count, norms, fast, leaf_local, charges, points, basis, field,
    buf, charge_buf, point_buf, local_buf, basis_buf, in_sem, out_sem, sem,
):
    fits = jnp.max(norms[...]) <= EXTENT
    bad = jnp.max(jnp.where(norms[...] <= EXTENT, 0.0, 1.0)) > 0.0
    direct = jnp.logical_or(bad, jnp.logical_not(fits))

    def cols(leaf):
        return pl.ds(leaf * PTS, PTS)

    @pl.when(jnp.logical_not(direct))
    def _():
        reads = [
            pltpu.make_async_copy(fast.at[:, cols(i)], buf.at[i], in_sem.at[i]) for i in range(LEAF)
        ]
        writes = [
            pltpu.make_async_copy(buf.at[i], field.at[:, cols(i)], out_sem.at[i]) for i in range(LEAF)
        ]
        for copy in reads:
            copy.start()
        for read, write in zip(reads, writes):
            read.wait()
            write.start()
        for write in writes:
            write.wait()

    @pl.when(direct)
    def _():
        me = lax.axis_index("box")

        def fetch(src, dst):
            copy = pltpu.make_async_copy(src, dst, sem)
            copy.start()
            copy.wait()

        fetch(points, point_buf)
        fetch(leaf_local, local_buf)
        fetch(basis, basis_buf)

        def one(leaf, carry):
            buf[0] = lax.dot_general(
                local_buf[leaf], basis_buf[leaf], (((0,), (0,)), ((), ())), preferred_element_type=F32
            )
            target = point_buf[OWN + leaf]

            def pair(j, inner):
                slot = jnp.clip(near_list[leaf, j] - me * LEAF + OWN, 0, SLOTS - 1)
                fetch(charges.at[slot], charge_buf)
                column = point_buf[slot].T
                squared = SOFT
                for axis in range(3):
                    gap = column[:, axis : axis + 1] - target[axis : axis + 1]
                    squared = squared + gap * gap
                block = (INV * lax.rsqrt(squared)).astype(BF16)
                buf[0] += jnp.dot(charge_buf[...], block, preferred_element_type=F32)
                return inner

            lax.fori_loop(0, near_count[leaf], pair, 0)
            fetch(buf.at[0], field.at[:, pl.ds(pl.multiple_of(leaf * PTS, PTS), PTS)])
            return carry

        lax.fori_loop(0, LEAF, one, 0)


def result(*operands):
    any_spec = pl.BlockSpec(memory_space=pl.ANY)
    smem_spec = pl.BlockSpec(memory_space=pltpu.SMEM)
    vmem_spec = pl.BlockSpec(memory_space=pltpu.VMEM)
    return pl.pallas_call(
        result_kernel,
        out_shape=jax.ShapeDtypeStruct((RHS, LEAF * PTS), F32),
        in_specs=[smem_spec] * 2 + [vmem_spec] + [any_spec] * 5,
        out_specs=any_spec,
        scratch_shapes=[
            pltpu.VMEM((LEAF, RHS, PTS), F32),
            pltpu.VMEM((RHS, PTS), BF16),
            pltpu.VMEM((SLOTS, 3, PTS), F32),
            pltpu.VMEM((LEAF, RANK, RHS), BF16),
            pltpu.VMEM((LEAF, RANK, PTS), BF16),
            pltpu.SemaphoreType.DMA((LEAF,)),
            pltpu.SemaphoreType.DMA((LEAF,)),
            pltpu.SemaphoreType.DMA,
        ],
        name="result",
    )(*operands)


def on_device(
    sources, points, near_list, near_count, far_list, far_count,
    leaf_basis, leaf_transfer, leaf_coupling, branch_transfer, branch_coupling,
):
    devices = lax.axis_size("box")
    fast, leaf_local, norms, charges, window_points = tree(
        devices, near_list, near_count, far_list, far_count, sources, points,
        leaf_basis, leaf_transfer, leaf_coupling, branch_transfer, branch_coupling,
    )
    return result(
        near_list, near_count, norms, fast, leaf_local, charges, window_points, leaf_basis
    )


def solution(mesh):
    placed = (
        P(None, "box"),
        P(None, "box"),
        P("box", None),
        P("box"),
        P("box", None),
        P("box"),
        P("box", None, None),
        P("box", None, None),
        P("box", None, None),
        P("box", None, None, None),
        P("box", None, None, None),
    )
    return jax.shard_map(
        on_device, mesh=mesh, in_specs=placed, out_specs=P(None, "box"), check_vma=False
    )
```

time: 688 us -> 83.5 us (0.12)
  the two profiles are of different devices: /device:TPU:86 before, /device:TPU:16 now
where the time goes in v1:
time: 83.5 us; the launch traced here: 83.3 us
  Pallas kernels  81.9 us (98%)
  local copies, waits for them, and re-layouts  1.35 us (2%)
    pallas_call x1, Pallas kernels, tree(): pl.pallas_call(functools.partial(tree_kernel, devices), out_shape=(jax.Sh...  78.5 us
    pallas_call x1, Pallas kernels, result(): pl.pallas_call(result_kernel, out_shape=jax.ShapeDtypeStruct((RHS, LEAF *...  3.39 us

profile of v1, /device:TPU:16, one launch (start us, length us, event | category | flops | bytes accessed | tf_op | source)
XLA Modules:
  0.0 83.3 jit_solution(14237124581106606688)
XLA Ops:
  0.0 1.3 %copy.12.far_list = s32[8,4]{1,0:T(8,128)} copy(s32[8,4]{0,1:T(4,128)} %param.15) | data formatting | bytes 256 | tf_op args[4]
  1.3 78.5 %tree.1 = (f32[128,4096]{1,0:T(8,128)}, bf16[8,64,128]{2,1,0:T(8,128)(2,1)}, f32[32,512]{1,0:T(8,128)}, bf16[32,128,512]{2,1,0:T(8,128)(2,1)}, f32[32,3,512]{2,1,0:T(4,128)}) custom-call(s32[8,12]{1,0:T(8,128)} %near_list.3, s32[8]{0:T(128)} %near_count.3, s32[8,4]{1,0:T(8,128)} %copy.12.far_list, s32[8]{0:T(128)} %far_count.1, bf16[128,4096]{1,0:T(8,128)(2,1)} %sources.1, ...), custom_call_target="tpu_custom_call" | custom-call | tf_op jit(solution)/shard_map/tree/pallas_call | solution.py:417
  79.9 3.4 %result.1 = f32[128,4096]{1,0:T(8,128)} custom-call(s32[8,12]{1,0:T(8,128)} %near_list.3, s32[8]{0:T(128)} %near_count.3, f32[32,512]{1,0:T(8,128)} %get-tuple-element.10.norms, f32[128,4096]{1,0:T(8,128)} %get-tuple-element.11.fast, bf16[8,64,128]{2,1,0:T(8,128)(2,1)} %get-tuple-element.12.leaf_local, bf16[32,128,512]{2,1,0:T(8,128)(2,1)} %get-tuple-element.13.charges, ...), custom_call_target="tpu_custom_call" | custom-call | tf_op jit(solution)/shard_map/result/pallas_call | solution.py:529

commit v2 on v1

--- a/solution.py
+++ b/solution.py
@@ -25,31 +25,25 @@
 OWN = REACH
 UP = 6
 LEVELS = 7
-FEAT = 32
+FEAT = 48
 GROUP = 6
 MESH = pl.DeviceIdType.MESH
 
-WINDOW = (
-    (1, 6, 2, 0),
-    (-1, 0, 2, 0),
-    (1, 4, 2, 1),
-    (-1, 2, 2, 1),
-    (2, 4, 4, 2),
-    (-2, 0, 4, 2),
-    (1, 0, 4, 2),
-    (-1, 4, 4, 2),
-)
 EDGES = ((1, 0, 8), (-1, 0, 8), (2, 4, 4), (-2, 0, 4))
-N_WIN, N_EDGE = len(WINDOW), len(EDGES)
+N_EDGE = len(EDGES)
+NEST = 3
+PAIR = (6, 24, 40, 48, 56)
 I_PTS = 0
 I_MOM = I_PTS + N_EDGE
 I_WIN = I_MOM + N_EDGE
-I_SWAP = I_WIN + N_WIN
-I_FAR = I_SWAP + UP
+I_CORE = I_WIN + 5
+I_LINE = I_CORE + 1
+I_COLUMN = I_LINE + 3
+I_FAR = I_COLUMN + 7
 N_MSG = I_FAR + 3 * LEVELS
 
-UP_AT = (0, 1, 3, 5, 7, 10)
-FAR_AT = (11, 11, 12, 12, 13, 14)
+CORE_AT, LINE_AT, COLUMN_AT, PASS_AT = 0, 3, 8, 5
+FAR_AT = (9, 10, 14, 11, 14, 15)
 
 
 def split3(x):
@@ -63,32 +57,29 @@
     return jnp.concatenate(parts, axis=0)
 
 
-def source_features(x):
+def halves(x):
+    high = x.astype(BF16)
+    return high, (x - high.astype(F32)).astype(BF16)
+
+
+def features(x, of_source):
+    row = lax.broadcasted_iota(jnp.int32, x.shape, 0)
     n = jnp.sum(x * x, axis=0, keepdims=True)
-    a, b, c = split3(x)
-    n0, n1, n2 = split3(n + SOFT * SCALE * SCALE)
-    ones = jnp.ones((3, PTS), BF16)
-    return rows([a, b, a, b, c, a, n0, n1, n2, ones, jnp.zeros((FEAT - 24, PTS), BF16)]), n
-
-
-def target_features(x):
-    n = jnp.sum(x * x, axis=0, keepdims=True)
-    a, b, c = split3(-2.0 * x)
-    n0, n1, n2 = split3(n)
-    ones = jnp.ones((3, PTS), BF16)
-    return rows([a, a, b, b, a, c, ones, n0, n1, n2, jnp.zeros((FEAT - 24, PTS), BF16)])
-
-
-def exact_dot(left, right, contract=1):
-    high = right.astype(BF16)
-    low = (right - high.astype(F32)).astype(BF16)
-    both = lax.dot_general(
-        left,
-        jnp.concatenate([high, low], axis=1),
-        (((contract,), (0,)), ((), ())),
-        preferred_element_type=F32,
-    )
-    return both[:, :RHS] + both[:, RHS:]
+    a, b, c = (v.astype(F32) for v in split3(x if of_source else -2.0 * x))
+    n0, n1, n2 = (v.astype(F32) for v in split3(n + SOFT * SCALE * SCALE if of_source else n))
+    norm = jnp.where(row == 3, n0, jnp.where(row == 4, n1, jnp.where(row == 5, n2, 0.0)))
+    ones = jnp.where((row >= 3) & (row < 6), 1.0, 0.0)
+    if of_source:
+        parts = [a + norm, b + ones, a, b, c, a]
+    else:
+        parts = [a + ones, a + norm, b, b, a, c]
+    return rows(parts), n
+
+
+def exact_dot(left, right):
+    width = right.shape[1]
+    both = jnp.dot(left, jnp.concatenate(halves(right), axis=1), preferred_element_type=F32)
+    return both[:, :width] + both[:, width:]
 
 
 def tree_kernel(
@@ -113,15 +104,22 @@
     pts,
     moments,
     feats,
+    padded,
     kernels,
     basis,
     transfer,
     coupling,
     branch_t,
     branch_c,
+    ladder,
     level,
-    term,
-    swapped,
+    core_out,
+    core_in,
+    line_out,
+    line_in,
+    column_own,
+    column_out,
+    column_in,
     arrived,
     far,
     spread,
@@ -138,6 +136,12 @@
     def other(distance):
         return lax.rem(me + distance + devices, devices)
 
+    def flipped(pattern):
+        return lax.bitwise_xor(me, pattern)
+
+    odd_core = lax.rem(me, 2)
+    sibling = me + 1 - 2 * odd_core
+
     def third(height):
         odd = lax.rem(lax.div(me, 1 << height), 2)
         return other((3 - 6 * odd) * (1 << height))
@@ -155,6 +159,7 @@
     barrier = pltpu.get_barrier_semaphore()
     partners = [other(s * (1 << k)) for k in range(LEVELS) for s in (1, -1)]
     partners += [other(devices // 2)] + [third(h) for h in range(LEVELS)]
+    partners += [flipped(pattern) for pattern in PAIR]
     for partner in partners:
         pl.semaphore_signal(barrier, inc=1, device_id=(partner,), device_id_type=MESH)
 
@@ -186,27 +191,45 @@
         )
 
     def window(which):
-        distance, first, count, _ = WINDOW[which]
-        return remote(
-            I_WIN + which,
-            charges.at[pl.ds(OWN + first, count)],
-            charges.at[pl.ds(OWN + first - LEAF * distance, count)],
-            other(distance),
-        )
-
-    def window_stage(stage):
-        for which in range(N_WIN):
-            if WINDOW[which][3] == stage:
-                window(which).start()
-
-    def swap(height):
-        bit = lax.rem(lax.div(me, 1 << height), 2)
-        return remote(
-            I_SWAP + height,
-            term.at[height],
-            swapped.at[height],
-            me + (1 - 2 * bit) * (1 << height),
-        )
+        def four(index, first, there, device, count=4):
+            return remote(
+                I_WIN + index, charges.at[pl.ds(first, count)], charges.at[pl.ds(there, count)], device
+            )
+
+        if which == 0:
+            return four(0, OWN, 4 + 16 * odd_core, sibling, LEAF)
+        beyond = other(2 * odd_core - 1)
+        if which == 1:
+            return four(1, OWN + 4 * odd_core, 20 - 12 * odd_core, beyond)
+        if which == 2:
+            return four(2, OWN + 4 - 4 * odd_core, 24 - 20 * odd_core, beyond)
+        if which == 3:
+            return four(3, OWN + 4 - 4 * odd_core, 28 * odd_core, other(2 - 4 * odd_core))
+        return four(4, 8 + 12 * odd_core, 28 * odd_core, sibling)
+
+    def core_copy():
+        return remote(I_CORE, core_out, core_in, sibling)
+
+    def line_copies():
+        return [
+            remote(I_LINE, line_out, line_in.at[pl.ds(0, 2)], flipped(2)),
+            remote(I_LINE + 1, line_out.at[1], line_in.at[2], flipped(4)),
+            remote(I_LINE + 2, line_out.at[1], line_in.at[3], flipped(6)),
+        ]
+
+    def column_first(k):
+        return 0 if k == 1 else 1 if k < 4 else 2
+
+    def column_copies():
+        copies = []
+        for k in range(1, 8):
+            part = pl.ds(column_first(k), NEST - column_first(k))
+            copies.append(
+                remote(
+                    I_COLUMN + k - 1, column_out.at[part], column_in.at[k - 1, part], flipped(8 * k)
+                )
+            )
+        return copies
 
     def far_copies(height):
         step = 1 << height
@@ -231,33 +254,57 @@
         edge(I_PTS, pts, which).start()
     for copy in load_charges:
         copy.wait()
-    window_stage(0)
+    window(1).start()
+    window(0).start()
 
     load_basis.wait()
     load_transfer.wait()
+    load_branch_t.wait()
     for i in range(LEAF):
         moments[OWN + i] = lax.dot_general(
             basis[i], charges[OWN + i], (((1,), (1,)), ((), ())), preferred_element_type=F32
         ).astype(BF16)
-    level[0] = jnp.dot(
+    base = jnp.dot(
         transfer[...],
         moments[pl.ds(OWN, LEAF)].reshape(LEAF * RANK, RHS),
         preferred_element_type=F32,
     )
-    load_branch_t.wait()
-    term[0] = exact_dot(half(0), level[0])
-    swap(0).start()
+    for nest in range(2):
+        first, second, last = (half(NEST * nest + i) for i in range(NEST))
+        two = jnp.dot(second, first, preferred_element_type=F32)
+        three = exact_dot(last, two)
+        high, low = halves(rows([first.astype(F32), two, three]))
+        ladder[nest] = jnp.concatenate([high, low], axis=1)
+
+    def climb(nest, x):
+        high, low = halves(x)
+        pair = ladder[nest]
+        wide = jnp.concatenate([high, low], axis=1)
+        r = jnp.dot(pair[:, :RANK], wide, preferred_element_type=F32)
+        fine = jnp.dot(pair[:, RANK:], high, preferred_element_type=F32)
+        return (r[:, :RHS] + r[:, RHS:] + fine).reshape(NEST, RANK, RHS)
+
+    def descend(nest, x):
+        wide = jnp.concatenate(halves(x), axis=1)
+        r = lax.dot_general(
+            ladder[nest], wide, (((0,), (0,)), ((), ())), preferred_element_type=F32
+        )
+        return r[:RANK, :RHS] + r[:RANK, RHS:] + r[RANK:, :RHS]
+
+    core_out[...] = climb(0, base)
+    level[0] = base.astype(BF16)
+    core_copy().start()
     for which in range(N_EDGE):
         edge(I_MOM, moments, which).start()
     for copy in far_copies(0):
         copy.start()
 
     def prepare(slot):
-        x = pts[slot]
-        centred = (x - x[:, 0:1]) * SCALE
-        packed, own_norm = source_features(centred)
-        feats[slot] = packed.astype(F32).T.astype(BF16)
-        apart = (x - pts[OWN][:, 0:1]) * SCALE
+        x = rows([pts[slot], jnp.zeros((5, PTS), F32)])
+        padded[slot] = x
+        packed, own_norm = features((x - x[:, 0:1]) * SCALE, True)
+        feats[slot] = packed.T.astype(BF16)
+        apart = (x[0:3] - pts[OWN][:, 0:1]) * SCALE
         apart_norm = jnp.sum(apart * apart, axis=0, keepdims=True) * FAR_SCALE
         norms[pl.ds(slot, 1)] = jnp.maximum(own_norm, apart_norm)
 
@@ -277,22 +324,54 @@
 
     def build(leaf, column):
         slot = slot_of(near_list[leaf, column])
-        target = (pts[OWN + leaf] - pts[slot][:, 0:1]) * SCALE
-        squared = jnp.dot(feats[slot], target_features(target), preferred_element_type=F32)
+        target = (padded[OWN + leaf] - padded[slot][:, 0:1]) * SCALE
+        packed, _ = features(target, False)
+        squared = jnp.dot(feats[slot], packed.astype(BF16), preferred_element_type=F32)
         kernels[leaf * NEAR + column] = lax.rsqrt(
             jnp.maximum(squared, SOFT * SCALE * SCALE)
         ).astype(BF16)
 
-    def up_step(height):
-        swap(height).wait_recv()
-        level[height + 1] = term[height] + swapped[height]
-        if height + 1 < UP:
-            term[height + 1] = exact_dot(half(height + 1), level[height + 1])
-            swap(height + 1).start()
-        for copy in far_copies(height + 1):
+    def core_step():
+        core_copy().wait_recv()
+        level[1] = (core_out[0] + core_in[0]).astype(BF16)
+        line_out[...] = core_out[pl.ds(1, 2)] + core_in[pl.ds(1, 2)]
+        for copy in line_copies():
             copy.start()
-        if height < 2:
-            window_stage(height + 1)
+        window(2).start()
+        window(3).start()
+        for copy in far_copies(1):
+            copy.start()
+
+    def line_step():
+        for copy in line_copies():
+            copy.wait_recv()
+        level[2] = (line_out[0] + line_in[0]).astype(BF16)
+        third_level = (line_out[1] + line_in[1]) + (line_in[2] + line_in[3])
+        level[3] = third_level.astype(BF16)
+        column_own[...] = climb(1, third_level)
+        column_out[...] = column_own[...].astype(BF16)
+        for copy in column_copies():
+            copy.start()
+        for height in (2, 3):
+            for copy in far_copies(height):
+                copy.start()
+
+    def column_step():
+        for copy in column_copies():
+            copy.wait_recv()
+        for i in range(NEST):
+            total = column_own[i]
+            for k in range(1, 8):
+                if column_first(k) <= i:
+                    total += column_in[k - 1, i].astype(F32)
+            level[NEST + 1 + i] = total.astype(BF16)
+        for height in (6, 5, 4):
+            for copy in far_copies(height):
+                copy.start()
+
+    def pass_step():
+        window(1).wait_recv()
+        window(4).start()
 
     def far_step(height):
         for copy in far_copies(height):
@@ -302,7 +381,8 @@
         odd = lax.rem(index, 2)
 
         def kept(slot, usable):
-            return jnp.where(usable, arrived[height, slot], 0.0)
+            block = arrived[height, slot]
+            return jnp.where(usable, block, jnp.zeros_like(block))
 
         last = 0 if height == LEVELS - 1 else 1
         stack = rows(
@@ -313,18 +393,25 @@
                 kept(2, (odd == 0) & (index + 3 < total)),
             ]
         )
-        far[height] = exact_dot(branch_c[height], stack)
+        far[pl.ds(height * RANK, RANK)] = jnp.dot(
+            branch_c[height], stack, preferred_element_type=F32
+        )
 
     def near_group(group, carry):
         leaf = lax.div(group, NEAR // GROUP)
         first = lax.rem(group, NEAR // GROUP) * GROUP
         for u in range(GROUP):
             build(leaf, first + u)
-        for height, at in enumerate(UP_AT):
+        for step, at in (
+            (core_step, CORE_AT),
+            (line_step, LINE_AT),
+            (pass_step, PASS_AT),
+            (column_step, COLUMN_AT),
+        ):
 
             @pl.when(group == at)
             def _():
-                up_step(height)
+                step()
 
         for height, at in enumerate(FAR_AT):
 
@@ -339,14 +426,18 @@
     lax.fori_loop(0, LEAF * NEAR // GROUP, near_group, 0)
 
     far_step(LEVELS - 1)
-    local = far[LEVELS - 1]
-    for height in range(UP - 1, -1, -1):
-        local = far[height] + exact_dot(half(height), local, 0)
-    spread[...] = exact_dot(transfer[...], local, 0).reshape(LEAF, RANK, RHS)
+    upper = descend(1, far[pl.ds((NEST + 1) * RANK, NEST * RANK)])
+    far[pl.ds(NEST * RANK, RANK)] += upper
+    local = far[pl.ds(0, RANK)] + descend(0, far[pl.ds(RANK, NEST * RANK)])
+    wide = jnp.concatenate(halves(local), axis=1)
+    spread_both = lax.dot_general(
+        transfer[...], wide, (((0,), (0,)), ((), ())), preferred_element_type=F32
+    )
+    spread[...] = (spread_both[:, :RHS] + spread_both[:, RHS:]).reshape(LEAF, RANK, RHS)
     load_coupling.wait()
     for which in range(N_EDGE):
         edge(I_MOM, moments, which).wait_recv()
-    for which in range(N_WIN):
+    for which in (0, 2, 3, 4):
         window(which).wait_recv()
     keep = [
         pltpu.make_async_copy(charges, charges_out, store_sem.at[2]),
@@ -364,7 +455,7 @@
     def finish(leaf, buf):
         blocks = []
         for j in range(FAR):
-            block = moments[slot_of(far_list[leaf, j])]
+            block = moments[slot_of(far_list[j, leaf])]
             blocks.append(jnp.where(j < far_count[leaf], block.astype(F32), 0.0).astype(BF16))
         here = jnp.dot(coupling[leaf], rows(blocks), preferred_element_type=F32) + spread[leaf]
         here = here.astype(BF16)
@@ -399,10 +490,10 @@
     for which in range(N_EDGE):
         edge(I_PTS, pts, which).wait_send()
         edge(I_MOM, moments, which).wait_send()
-    for which in range(N_WIN):
+    for which in range(5):
         window(which).wait_send()
-    for height in range(UP):
-        swap(height).wait_send()
+    for copy in [core_copy()] + line_copies() + column_copies():
+        copy.wait_send()
     for height in range(LEVELS):
         for copy in far_copies(height):
             copy.wait_send()
@@ -430,17 +521,24 @@
             pltpu.VMEM((SLOTS, 3, PTS), F32),
             pltpu.VMEM((SLOTS, RANK, RHS), BF16),
             pltpu.VMEM((SLOTS, PTS, FEAT), BF16),
+            pltpu.VMEM((SLOTS, 8, PTS), F32),
             pltpu.VMEM((LEAF * NEAR, PTS, PTS), BF16),
             pltpu.VMEM((LEAF, RANK, PTS), BF16),
             pltpu.VMEM((RANK, LEAF * RANK), BF16),
             pltpu.VMEM((LEAF, RANK, FAR * RANK), BF16),
             pltpu.VMEM((UP, RANK, 2 * RANK), BF16),
             pltpu.VMEM((LEVELS, RANK, 4 * RANK), BF16),
-            pltpu.VMEM((LEVELS, RANK, RHS), F32),
-            pltpu.VMEM((UP, RANK, RHS), F32),
-            pltpu.VMEM((UP, RANK, RHS), F32),
-            pltpu.VMEM((LEVELS, 3, RANK, RHS), F32),
-            pltpu.VMEM((LEVELS, RANK, RHS), F32),
+            pltpu.VMEM((2, NEST * RANK, 2 * RANK), BF16),
+            pltpu.VMEM((LEVELS, RANK, RHS), BF16),
+            pltpu.VMEM((NEST, RANK, RHS), F32),
+            pltpu.VMEM((NEST, RANK, RHS), F32),
+            pltpu.VMEM((2, RANK, RHS), F32),
+            pltpu.VMEM((4, RANK, RHS), F32),
+            pltpu.VMEM((NEST, RANK, RHS), F32),
+            pltpu.VMEM((NEST, RANK, RHS), BF16),
+            pltpu.VMEM((7, NEST, RANK, RHS), BF16),
+            pltpu.VMEM((LEVELS, 3, RANK, RHS), BF16),
+            pltpu.VMEM((LEVELS * RANK, RHS), F32),
             pltpu.VMEM((LEAF, RANK, RHS), F32),
             pltpu.VMEM((SLOTS, PTS), F32),
             pltpu.VMEM((LEAF, RANK, RHS), BF16),
@@ -459,25 +557,26 @@
 
 def result_kernel(
     near_list, near_count, norms, fast, leaf_local, charges, points, basis, field,
-    buf, charge_buf, point_buf, local_buf, basis_buf, in_sem, out_sem, sem,
+    buf, charge_buf, point_buf, local_buf, basis_buf, norm_buf, in_sem, out_sem, sem,
 ):
-    fits = jnp.max(norms[...]) <= EXTENT
-    bad = jnp.max(jnp.where(norms[...] <= EXTENT, 0.0, 1.0)) > 0.0
-    direct = jnp.logical_or(bad, jnp.logical_not(fits))
-
     def cols(leaf):
         return pl.ds(leaf * PTS, PTS)
 
+    reads = [
+        pltpu.make_async_copy(fast.at[:, cols(i)], buf.at[i], in_sem.at[i]) for i in range(LEAF)
+    ]
+    writes = [
+        pltpu.make_async_copy(buf.at[i], field.at[:, cols(i)], out_sem.at[i]) for i in range(LEAF)
+    ]
+    get_norms = pltpu.make_async_copy(norms, norm_buf, sem)
+    get_norms.start()
+    for copy in reads:
+        copy.start()
+    get_norms.wait()
+    direct = jnp.max(jnp.where(norm_buf[...] <= EXTENT, 0.0, 1.0)) > 0.0
+
     @pl.when(jnp.logical_not(direct))
     def _():
-        reads = [
-            pltpu.make_async_copy(fast.at[:, cols(i)], buf.at[i], in_sem.at[i]) for i in range(LEAF)
-        ]
-        writes = [
-            pltpu.make_async_copy(buf.at[i], field.at[:, cols(i)], out_sem.at[i]) for i in range(LEAF)
-        ]
-        for copy in reads:
-            copy.start()
         for read, write in zip(reads, writes):
             read.wait()
             write.start()
@@ -487,6 +586,8 @@
     @pl.when(direct)
     def _():
         me = lax.axis_index("box")
+        for read in reads:
+            read.wait()
 
         def fetch(src, dst):
             copy = pltpu.make_async_copy(src, dst, sem)
@@ -525,11 +626,10 @@
 def result(*operands):
     any_spec = pl.BlockSpec(memory_space=pl.ANY)
     smem_spec = pl.BlockSpec(memory_space=pltpu.SMEM)
-    vmem_spec = pl.BlockSpec(memory_space=pltpu.VMEM)
     return pl.pallas_call(
         result_kernel,
         out_shape=jax.ShapeDtypeStruct((RHS, LEAF * PTS), F32),
-        in_specs=[smem_spec] * 2 + [vmem_spec] + [any_spec] * 5,
+        in_specs=[smem_spec] * 2 + [any_spec] * 6,
         out_specs=any_spec,
         scratch_shapes=[
             pltpu.VMEM((LEAF, RHS, PTS), F32),
@@ -537,6 +637,7 @@
             pltpu.VMEM((SLOTS, 3, PTS), F32),
             pltpu.VMEM((LEAF, RANK, RHS), BF16),
             pltpu.VMEM((LEAF, RANK, PTS), BF16),
+            pltpu.VMEM((SLOTS, PTS), F32),
             pltpu.SemaphoreType.DMA((LEAF,)),
             pltpu.SemaphoreType.DMA((LEAF,)),
             pltpu.SemaphoreType.DMA,
@@ -551,7 +652,7 @@
 ):
     devices = lax.axis_size("box")
     fast, leaf_local, norms, charges, window_points = tree(
-        devices, near_list, near_count, far_list, far_count, sources, points,
+        devices, near_list, near_count, far_list.T, far_count, sources, points,
         leaf_basis, leaf_transfer, leaf_coupling, branch_transfer, branch_coupling,
     )
     return result(

time: 83.5 us -> 72.5 us (0.87)
  the two profiles are of different devices: /device:TPU:16 before, /device:TPU:1 now
where the time goes in v2:
time: 72.5 us; the launch traced here: 72.3 us
  Pallas kernels  72.3 us (100%)
    pallas_call x1, Pallas kernels, tree(): pl.pallas_call(functools.partial(tree_kernel, devices), out_shape=(jax.Sh...  68.6 us
    pallas_call x1, Pallas kernels, result(): pl.pallas_call(result_kernel, out_shape=jax.ShapeDtypeStruct((RHS, LEAF *...  3.72 us

profile of v2, /device:TPU:1, one launch (start us, length us, event | category | flops | bytes accessed | tf_op | source)
XLA Modules:
  0.0 72.3 jit_solution(559003843433976214)
XLA Ops:
  0.0 68.6 %tree.1 = (f32[128,4096]{1,0:T(8,128)}, bf16[8,64,128]{2,1,0:T(8,128)(2,1)}, f32[32,512]{1,0:T(8,128)}, bf16[32,128,512]{2,1,0:T(8,128)(2,1)}, f32[32,3,512]{2,1,0:T(4,128)}) custom-call(s32[8,12]{1,0:T(8,128)} %near_list.3, s32[8]{0:T(128)} %near_count.3, s32[4,8]{1,0:T(4,128)} %bitcast.1, s32[8]{0:T(128)} %far_count.1, bf16[128,4096]{1,0:T(8,128)(2,1)} %sources.1, ...), custom_call_target="tpu_custom_call" | custom-call | tf_op jit(solution)/shard_map/tree/pallas_call | solution.py:508
  68.6 3.7 %result.1 = f32[128,4096]{1,0:T(8,128)} custom-call(s32[8,12]{1,0:T(8,128)} %near_list.3, s32[8]{0:T(128)} %near_count.3, f32[32,512]{1,0:T(8,128)} %get-tuple-element.10.norms, f32[128,4096]{1,0:T(8,128)} %get-tuple-element.11.fast, bf16[8,64,128]{2,1,0:T(8,128)(2,1)} %get-tuple-element.12.leaf_local, bf16[32,128,512]{2,1,0:T(8,128)(2,1)} %get-tuple-element.13.charges, ...), custom_call_target="tpu_custom_call" | custom-call | tf_op jit(solution)/shard_map/result/pallas_call | solution.py:629

commit v3 on v2

--- a/solution.py
+++ b/solution.py
@@ -36,14 +36,16 @@
 I_PTS = 0
 I_MOM = I_PTS + N_EDGE
 I_WIN = I_MOM + N_EDGE
-I_CORE = I_WIN + 5
+N_WIN = 14
+I_CORE = I_WIN + N_WIN
 I_LINE = I_CORE + 1
 I_COLUMN = I_LINE + 3
 I_FAR = I_COLUMN + 7
 N_MSG = I_FAR + 3 * LEVELS
 
-CORE_AT, LINE_AT, COLUMN_AT, PASS_AT = 0, 3, 8, 5
-FAR_AT = (9, 10, 14, 11, 14, 15)
+LINE_AT, PASS_AT, COLUMN_AT, MOMENTS_AT, DOWN_AT = 0, 4, 5, 8, 15
+FAR_AT = (6, 7, 10, 8, 11, 12, 13)
+CHARGES_FROM, CHARGES_TO = 0, 8
 
 
 def split3(x):
@@ -191,21 +193,34 @@
         )
 
     def window(which):
-        def four(index, first, there, device, count=4):
+        if which == 0:
             return remote(
-                I_WIN + index, charges.at[pl.ds(first, count)], charges.at[pl.ds(there, count)], device
+                I_WIN,
+                charges.at[pl.ds(OWN, LEAF)],
+                charges.at[pl.ds(4 + 16 * odd_core, LEAF)],
+                sibling,
             )
-
-        if which == 0:
-            return four(0, OWN, 4 + 16 * odd_core, sibling, LEAF)
-        beyond = other(2 * odd_core - 1)
-        if which == 1:
-            return four(1, OWN + 4 * odd_core, 20 - 12 * odd_core, beyond)
-        if which == 2:
-            return four(2, OWN + 4 - 4 * odd_core, 24 - 20 * odd_core, beyond)
-        if which == 3:
-            return four(3, OWN + 4 - 4 * odd_core, 28 * odd_core, other(2 - 4 * odd_core))
-        return four(4, 8 + 12 * odd_core, 28 * odd_core, sibling)
+        first, there = 8 + 12 * odd_core, 28 * odd_core
+        return remote(
+            I_WIN + 1, charges.at[pl.ds(first, 4)], charges.at[pl.ds(there, 4)], sibling
+        )
+
+    def ahead(k):
+        leaf = lax.rem(k + 4 * odd_core, LEAF)
+        return remote(
+            I_WIN + 2 + k,
+            charges.at[pl.ds(OWN + leaf, 1)],
+            charges.at[pl.ds(leaf + 20 - 16 * odd_core, 1)],
+            other(2 * odd_core - 1),
+        )
+
+    def behind(k):
+        return remote(
+            I_WIN + 10 + k,
+            charges.at[pl.ds(OWN + 4 - 4 * odd_core + k, 1)],
+            charges.at[pl.ds(28 * odd_core + k, 1)],
+            other(2 - 4 * odd_core),
+        )
 
     def core_copy():
         return remote(I_CORE, core_out, core_in, sibling)
@@ -254,7 +269,8 @@
         edge(I_PTS, pts, which).start()
     for copy in load_charges:
         copy.wait()
-    window(1).start()
+    ahead(0).start()
+    ahead(1).start()
     window(0).start()
 
     load_basis.wait()
@@ -294,10 +310,15 @@
     core_out[...] = climb(0, base)
     level[0] = base.astype(BF16)
     core_copy().start()
-    for which in range(N_EDGE):
-        edge(I_MOM, moments, which).start()
-    for copy in far_copies(0):
-        copy.start()
+    ahead(2).start()
+    ahead(3).start()
+
+    def core_step():
+        core_copy().wait_recv()
+        level[1] = (core_out[0] + core_in[0]).astype(BF16)
+        line_out[...] = core_out[pl.ds(1, 2)] + core_in[pl.ds(1, 2)]
+        for copy in line_copies():
+            copy.start()
 
     def prepare(slot):
         x = rows([pts[slot], jnp.zeros((5, PTS), F32)])
@@ -314,6 +335,7 @@
         return carry
 
     lax.fori_loop(OWN // 2, (OWN + LEAF) // 2, prepare_pair, 0)
+    core_step()
     for which in range(N_EDGE):
         edge(I_PTS, pts, which).wait_recv()
     lax.fori_loop(0, OWN // 2, prepare_pair, 0)
@@ -330,17 +352,6 @@
         kernels[leaf * NEAR + column] = lax.rsqrt(
             jnp.maximum(squared, SOFT * SCALE * SCALE)
         ).astype(BF16)
-
-    def core_step():
-        core_copy().wait_recv()
-        level[1] = (core_out[0] + core_in[0]).astype(BF16)
-        line_out[...] = core_out[pl.ds(1, 2)] + core_in[pl.ds(1, 2)]
-        for copy in line_copies():
-            copy.start()
-        window(2).start()
-        window(3).start()
-        for copy in far_copies(1):
-            copy.start()
 
     def line_step():
         for copy in line_copies():
@@ -352,7 +363,7 @@
         column_out[...] = column_own[...].astype(BF16)
         for copy in column_copies():
             copy.start()
-        for height in (2, 3):
+        for height in (3, 2, 1, 0):
             for copy in far_copies(height):
                 copy.start()
 
@@ -370,8 +381,13 @@
                 copy.start()
 
     def pass_step():
-        window(1).wait_recv()
-        window(4).start()
+        for k in range(4):
+            ahead(k).wait_recv()
+        window(1).start()
+
+    def moments_step():
+        for which in range(N_EDGE):
+            edge(I_MOM, moments, which).start()
 
     def far_step(height):
         for copy in far_copies(height):
@@ -397,16 +413,35 @@
             branch_c[height], stack, preferred_element_type=F32
         )
 
+    def down_step():
+        upper = descend(1, far[pl.ds((NEST + 1) * RANK, NEST * RANK)])
+        far[pl.ds(NEST * RANK, RANK)] += upper
+        local = far[pl.ds(0, RANK)] + descend(0, far[pl.ds(RANK, NEST * RANK)])
+        wide = jnp.concatenate(halves(local), axis=1)
+        spread_both = lax.dot_general(
+            transfer[...], wide, (((0,), (0,)), ((), ())), preferred_element_type=F32
+        )
+        spread[...] = (spread_both[:, :RHS] + spread_both[:, RHS:]).reshape(LEAF, RANK, RHS)
+
     def near_group(group, carry):
         leaf = lax.div(group, NEAR // GROUP)
         first = lax.rem(group, NEAR // GROUP) * GROUP
         for u in range(GROUP):
             build(leaf, first + u)
+        @pl.when((group >= CHARGES_FROM) & (group < CHARGES_FROM + 4))
+        def _():
+            ahead(4 + group - CHARGES_FROM).start()
+
+        @pl.when((group >= CHARGES_FROM + 4) & (group < CHARGES_TO))
+        def _():
+            behind(group - CHARGES_FROM - 4).start()
+
         for step, at in (
-            (core_step, CORE_AT),
             (line_step, LINE_AT),
             (pass_step, PASS_AT),
             (column_step, COLUMN_AT),
+            (moments_step, MOMENTS_AT),
+            (down_step, DOWN_AT),
         ):
 
             @pl.when(group == at)
@@ -425,20 +460,14 @@
 
     lax.fori_loop(0, LEAF * NEAR // GROUP, near_group, 0)
 
-    far_step(LEVELS - 1)
-    upper = descend(1, far[pl.ds((NEST + 1) * RANK, NEST * RANK)])
-    far[pl.ds(NEST * RANK, RANK)] += upper
-    local = far[pl.ds(0, RANK)] + descend(0, far[pl.ds(RANK, NEST * RANK)])
-    wide = jnp.concatenate(halves(local), axis=1)
-    spread_both = lax.dot_general(
-        transfer[...], wide, (((0,), (0,)), ((), ())), preferred_element_type=F32
-    )
-    spread[...] = (spread_both[:, :RHS] + spread_both[:, RHS:]).reshape(LEAF, RANK, RHS)
     load_coupling.wait()
     for which in range(N_EDGE):
         edge(I_MOM, moments, which).wait_recv()
-    for which in (0, 2, 3, 4):
-        window(which).wait_recv()
+    window(0).wait_recv()
+    window(1).wait_recv()
+    for k in range(4):
+        ahead(4 + k).wait_recv()
+        behind(k).wait_recv()
     keep = [
         pltpu.make_async_copy(charges, charges_out, store_sem.at[2]),
         pltpu.make_async_copy(pts, points_out, store_sem.at[3]),
@@ -490,8 +519,12 @@
     for which in range(N_EDGE):
         edge(I_PTS, pts, which).wait_send()
         edge(I_MOM, moments, which).wait_send()
-    for which in range(5):
-        window(which).wait_send()
+    window(0).wait_send()
+    window(1).wait_send()
+    for k in range(8):
+        ahead(k).wait_send()
+    for k in range(4):
+        behind(k).wait_send()
     for copy in [core_copy()] + line_copies() + column_copies():
         copy.wait_send()
     for height in range(LEVELS):

time: 72.5 us -> 64.2 us (0.89)
  Pallas kernels: 72.3 us -> 64 us
    pallas_call x1, Pallas kernels: 68.6 us -> 60.3 us  [tree(): pl.pallas_call(functools.partial(tree_kernel, devices), out_shape=(jax.Sh...]
where the time goes in v3:
time: 64.2 us; the launch traced here: 64 us
  Pallas kernels  64 us (100%)
    pallas_call x1, Pallas kernels, tree(): pl.pallas_call(functools.partial(tree_kernel, devices), out_shape=(jax.Sh...  60.3 us
    pallas_call x1, Pallas kernels, result(): pl.pallas_call(result_kernel, out_shape=jax.ShapeDtypeStruct((RHS, LEAF *...  3.72 us

profile of v3, /device:TPU:1, one launch (start us, length us, event | category | flops | bytes accessed | tf_op | source)
XLA Modules:
  0.0 64.0 jit_solution(14671660336633535509)
XLA Ops:
  0.0 60.3 %tree.1 = (f32[128,4096]{1,0:T(8,128)}, bf16[8,64,128]{2,1,0:T(8,128)(2,1)}, f32[32,512]{1,0:T(8,128)}, bf16[32,128,512]{2,1,0:T(8,128)(2,1)}, f32[32,3,512]{2,1,0:T(4,128)}) custom-call(s32[8,12]{1,0:T(8,128)} %near_list.3, s32[8]{0:T(128)} %near_count.3, s32[4,8]{1,0:T(4,128)} %bitcast.1, s32[8]{0:T(128)} %far_count.1, bf16[128,4096]{1,0:T(8,128)(2,1)} %sources.1, ...), custom_call_target="tpu_custom_call" | custom-call | tf_op jit(solution)/shard_map/tree/pallas_call | solution.py:541
  60.3 3.7 %result.1 = f32[128,4096]{1,0:T(8,128)} custom-call(s32[8,12]{1,0:T(8,128)} %near_list.3, s32[8]{0:T(128)} %near_count.3, f32[32,512]{1,0:T(8,128)} %get-tuple-element.10.norms, f32[128,4096]{1,0:T(8,128)} %get-tuple-element.11.fast, bf16[8,64,128]{2,1,0:T(8,128)(2,1)} %get-tuple-element.12.leaf_local, bf16[32,128,512]{2,1,0:T(8,128)(2,1)} %get-tuple-element.13.charges, ...), custom_call_target="tpu_custom_call" | custom-call | tf_op jit(solution)/shard_map/result/pallas_call | solution.py:662

commit v4 on v3

--- a/solution.py
+++ b/solution.py
@@ -26,7 +26,7 @@
 UP = 6
 LEVELS = 7
 FEAT = 48
-GROUP = 6
+GROUP = 12
 MESH = pl.DeviceIdType.MESH
 
 EDGES = ((1, 0, 8), (-1, 0, 8), (2, 4, 4), (-2, 0, 4))
@@ -43,9 +43,8 @@
 I_FAR = I_COLUMN + 7
 N_MSG = I_FAR + 3 * LEVELS
 
-LINE_AT, PASS_AT, COLUMN_AT, MOMENTS_AT, DOWN_AT = 0, 4, 5, 8, 15
-FAR_AT = (6, 7, 10, 8, 11, 12, 13)
-CHARGES_FROM, CHARGES_TO = 0, 8
+LINE_AT, PASS_AT, COLUMN_AT, MOMENTS_AT, DOWN_AT = 0, 2, 2, 5, 7
+FAR_AT = (3, 3, 5, 4, 5, 6, 6)
 
 
 def split3(x):
@@ -428,13 +427,19 @@
         first = lax.rem(group, NEAR // GROUP) * GROUP
         for u in range(GROUP):
             build(leaf, first + u)
-        @pl.when((group >= CHARGES_FROM) & (group < CHARGES_FROM + 4))
+        @pl.when(group < 2)
         def _():
-            ahead(4 + group - CHARGES_FROM).start()
-
-        @pl.when((group >= CHARGES_FROM + 4) & (group < CHARGES_TO))
+            ahead(4 + group).start()
+
+        @pl.when(group == 2)
         def _():
-            behind(group - CHARGES_FROM - 4).start()
+            ahead(6).start()
+            ahead(7).start()
+
+        @pl.when((group >= 3) & (group < 5))
+        def _():
+            behind(2 * group - 6).start()
+            behind(2 * group - 5).start()
 
         for step, at in (
             (line_step, LINE_AT),
@@ -489,14 +494,14 @@
         here = jnp.dot(coupling[leaf], rows(blocks), preferred_element_type=F32) + spread[leaf]
         here = here.astype(BF16)
         leaf_local[leaf] = here
-        total = lax.dot_general(
-            here, basis[leaf], (((0,), (0,)), ((), ())), preferred_element_type=F32
-        )
+        total = jnp.zeros((RHS, PTS), F32)
         for j in range(NEAR):
             block = charges[slot_of(near_list[leaf, j])]
             block = jnp.where(j < near_count[leaf], block, jnp.zeros_like(block))
             total += jnp.dot(block, kernels[leaf * NEAR + j], preferred_element_type=F32)
-        out_buf[buf] = total
+        out_buf[buf] = total + lax.dot_general(
+            here, basis[leaf], (((0,), (0,)), ((), ())), preferred_element_type=F32
+        )
         out_copy(leaf, buf).start()
 
     def finish_pair(i, carry):

time: 64.2 us -> 62.4 us (0.972); the launches traced: 64 us -> 61.5 us
  Pallas kernels: 64 us -> 61.5 us
    pallas_call x1, Pallas kernels: 60.3 us -> 57.8 us  [tree(): pl.pallas_call(functools.partial(tree_kernel, devices), out_shape=(jax.Sh...]
where the time goes in v4:
time: 62.4 us; the launch traced here: 61.5 us
  Pallas kernels  61.5 us (99%)
    pallas_call x1, Pallas kernels, tree(): pl.pallas_call(functools.partial(tree_kernel, devices), out_shape=(jax.Sh...  57.8 us
    pallas_call x1, Pallas kernels, result(): pl.pallas_call(result_kernel, out_shape=jax.ShapeDtypeStruct((RHS, LEAF *...  3.72 us

profile of v4, /device:TPU:1, one launch (start us, length us, event | category | flops | bytes accessed | tf_op | source)
XLA Modules:
  0.0 61.5 jit_solution(14416913402127427686)
XLA Ops:
  0.0 57.8 %tree.1 = (f32[128,4096]{1,0:T(8,128)}, bf16[8,64,128]{2,1,0:T(8,128)(2,1)}, f32[32,512]{1,0:T(8,128)}, bf16[32,128,512]{2,1,0:T(8,128)(2,1)}, f32[32,3,512]{2,1,0:T(4,128)}) custom-call(s32[8,12]{1,0:T(8,128)} %near_list.3, s32[8]{0:T(128)} %near_count.3, s32[4,8]{1,0:T(4,128)} %bitcast.1, s32[8]{0:T(128)} %far_count.1, bf16[128,4096]{1,0:T(8,128)(2,1)} %sources.1, ...), custom_call_target="tpu_custom_call" | custom-call | tf_op jit(solution)/shard_map/tree/pallas_call | solution.py:546
  57.8 3.7 %result.1 = f32[128,4096]{1,0:T(8,128)} custom-call(s32[8,12]{1,0:T(8,128)} %near_list.3, s32[8]{0:T(128)} %near_count.3, f32[32,512]{1,0:T(8,128)} %get-tuple-element.10.norms, f32[128,4096]{1,0:T(8,128)} %get-tuple-element.11.fast, bf16[8,64,128]{2,1,0:T(8,128)(2,1)} %get-tuple-element.12.leaf_local, bf16[32,128,512]{2,1,0:T(8,128)(2,1)} %get-tuple-element.13.charges, ...), custom_call_target="tpu_custom_call" | custom-call | tf_op jit(solution)/shard_map/result/pallas_call | solution.py:667

commit v5 on v4

--- a/solution.py
+++ b/solution.py
@@ -263,6 +263,21 @@
 
     for copy in load_points:
         copy.wait()
+    def prepare(slot):
+        x = rows([pts[slot], jnp.zeros((5, PTS), F32)])
+        padded[slot] = x
+        packed, own_norm = features((x - x[:, 0:1]) * SCALE, True)
+        feats[slot] = packed.T.astype(BF16)
+        apart = (x[0:3] - pts[OWN][:, 0:1]) * SCALE
+        apart_norm = jnp.sum(apart * apart, axis=0, keepdims=True) * FAR_SCALE
+        norms[pl.ds(slot, 1)] = jnp.maximum(own_norm, apart_norm)
+
+    def prepare_pair(i, carry):
+        prepare(2 * i)
+        prepare(2 * i + 1)
+        return carry
+
+    lax.fori_loop(OWN // 2, (OWN + LEAF) // 2, prepare_pair, 0)
     pl.semaphore_wait(barrier, len(partners))
     for which in range(N_EDGE):
         edge(I_PTS, pts, which).start()
@@ -319,21 +334,6 @@
         for copy in line_copies():
             copy.start()
 
-    def prepare(slot):
-        x = rows([pts[slot], jnp.zeros((5, PTS), F32)])
-        padded[slot] = x
-        packed, own_norm = features((x - x[:, 0:1]) * SCALE, True)
-        feats[slot] = packed.T.astype(BF16)
-        apart = (x[0:3] - pts[OWN][:, 0:1]) * SCALE
-        apart_norm = jnp.sum(apart * apart, axis=0, keepdims=True) * FAR_SCALE
-        norms[pl.ds(slot, 1)] = jnp.maximum(own_norm, apart_norm)
-
-    def prepare_pair(i, carry):
-        prepare(2 * i)
-        prepare(2 * i + 1)
-        return carry
-
-    lax.fori_loop(OWN // 2, (OWN + LEAF) // 2, prepare_pair, 0)
     core_step()
     for which in range(N_EDGE):
         edge(I_PTS, pts, which).wait_recv()

time: 62.4 us -> 62.4 us (level)
  no operation moved by 1% of the time
where the time goes in v5:
time: 62.4 us; the launch traced here: 61.5 us
  Pallas kernels  61.5 us (99%)
    pallas_call x1, Pallas kernels, tree(): pl.pallas_call(functools.partial(tree_kernel, devices), out_shape=(jax.Sh...  57.8 us
    pallas_call x1, Pallas kernels, result(): pl.pallas_call(result_kernel, out_shape=jax.ShapeDtypeStruct((RHS, LEAF *...  3.72 us

profile of v5, /device:TPU:1, one launch (start us, length us, event | category | flops | bytes accessed | tf_op | source)
XLA Modules:
  0.0 61.5 jit_solution(9589822332550758979)
XLA Ops:
  0.0 57.8 %tree.1 = (f32[128,4096]{1,0:T(8,128)}, bf16[8,64,128]{2,1,0:T(8,128)(2,1)}, f32[32,512]{1,0:T(8,128)}, bf16[32,128,512]{2,1,0:T(8,128)(2,1)}, f32[32,3,512]{2,1,0:T(4,128)}) custom-call(s32[8,12]{1,0:T(8,128)} %near_list.3, s32[8]{0:T(128)} %near_count.3, s32[4,8]{1,0:T(4,128)} %bitcast.1, s32[8]{0:T(128)} %far_count.1, bf16[128,4096]{1,0:T(8,128)(2,1)} %sources.1, ...), custom_call_target="tpu_custom_call" | custom-call | tf_op jit(solution)/shard_map/tree/pallas_call | solution.py:546
  57.8 3.7 %result.1 = f32[128,4096]{1,0:T(8,128)} custom-call(s32[8,12]{1,0:T(8,128)} %near_list.3, s32[8]{0:T(128)} %near_count.3, f32[32,512]{1,0:T(8,128)} %get-tuple-element.10.norms, f32[128,4096]{1,0:T(8,128)} %get-tuple-element.11.fast, bf16[8,64,128]{2,1,0:T(8,128)(2,1)} %get-tuple-element.12.leaf_local, bf16[32,128,512]{2,1,0:T(8,128)(2,1)} %get-tuple-element.13.charges, ...), custom_call_target="tpu_custom_call" | custom-call | tf_op jit(solution)/shard_map/result/pallas_call | solution.py:667
